TPU v7x, 32 devices: a whole 2x2x4 slice. The times are simulated.
32 devices in a mesh: rep: 8 (over y, x, core), fsdp: 4 (over z).
Axes of the slice: x: 2, y: 2, z: 4, core: 2. Of those that a mesh axis runs over, the one named last changes fastest.
Arguments:
- tokens: bfloat16 [8, 2048, 1088], P('rep', 'fsdp'), may hold values from -6 to 6
- w_qkv: bfloat16 [1088, 3264], P('fsdp'), may hold values from -0.1875 to 0.1875
- qv_bias: bfloat16 [2176], P('fsdp'), may hold values from -0.29882812 to 0.29882812
- w_out: bfloat16 [1088, 1088], P('fsdp'), may hold values from -1.5 to 1.5
- out_bias: bfloat16 [1088], P('fsdp'), may hold values from -1.796875 to 1.796875
- w_up: bfloat16 [1088, 4352], P('fsdp'), may hold values from -0.1875 to 0.1875
- up_bias: bfloat16 [4352], P('fsdp'), may hold values from -3 to 3
- w_down: bfloat16 [4352, 1088], P('fsdp'), may hold values from -0.09375 to 0.09375
- down_bias: bfloat16 [1088], P('fsdp'), may hold values from -1.796875 to 1.796875
- ln1_gain: bfloat16 [1088], P('fsdp'), may hold values from 0.099609375 to 1.8984375
- ln1_bias: bfloat16 [1088], P('fsdp'), may hold values from -3 to 3
- ln2_gain: bfloat16 [1088], P('fsdp'), may hold values from 0.099609375 to 1.8984375
- ln2_bias: bfloat16 [1088], P('fsdp'), may hold values from -3 to 3
- cotangent: bfloat16 [8, 2048, 1088], P('rep', 'fsdp'), may hold values from -6 to 6
Outputs:
- layer_out: float32 [8, 2048, 1088], P('rep', 'fsdp')
- grad_tokens: float32 [8, 2048, 1088], P('rep', 'fsdp')
- grad_w_qkv: float32 [1088, 3264], P('fsdp')
- grad_qv_bias: float32 [2176], P('fsdp')
- grad_w_out: float32 [1088, 1088], P('fsdp')
- grad_out_bias: float32 [1088], P('fsdp')
- grad_w_up: float32 [1088, 4352], P('fsdp')
- grad_up_bias: float32 [4352], P('fsdp')
- grad_w_down: float32 [4352, 1088], P('fsdp')
- grad_down_bias: float32 [1088], P('fsdp')
- grad_ln1_gain: float32 [1088], P('fsdp')
- grad_ln1_bias: float32 [1088], P('fsdp')
- grad_ln2_gain: float32 [1088], P('fsdp')
- grad_ln2_bias: float32 [1088], P('fsdp')
All inputs are finite; a program needn't handle non-finite values.
Results may differ from a plain program's by a relative error of at most 0.012.
Values may be sent and summed in bfloat16 or wider, within the bound.
No kernel may reach another device: no remote copies, remote signals or barrier semaphores. Data moves between devices by JAX's collectives and lax.ppermute only.
A program may use at most 256 MiB of HBM per device.

v0:
```python
import jax
import jax.numpy as jnp
from jax import lax
from jax.sharding import PartitionSpec as P

HD = 64


EPSILON = 1e-05


def normalize(vector):
    centre = vector - jnp.mean(vector, axis=-1, keepdims=True)
    inverse = lax.rsqrt(jnp.mean(centre * centre, axis=-1, keepdims=True) + EPSILON)
    return centre * inverse


def gelu_exact(vector):
    return jax.nn.gelu(vector, approximate=False)


def local(
    tokens,
    w_qkv,
    qv_bias,
    w_out,
    out_bias,
    w_up,
    up_bias,
    w_down,
    down_bias,
    ln1_gain,
    ln1_bias,
    ln2_gain,
    ln2_bias,
    cotangent,
):
    gathered = (
        lax.all_gather(w_qkv, "fsdp", axis=0, tiled=True),
        lax.all_gather(qv_bias, "fsdp", axis=0, tiled=True),
        lax.all_gather(w_out, "fsdp", axis=0, tiled=True),
        lax.all_gather(out_bias, "fsdp", axis=0, tiled=True),
        lax.all_gather(w_up, "fsdp", axis=0, tiled=True),
        lax.all_gather(up_bias, "fsdp", axis=0, tiled=True),
        lax.all_gather(w_down, "fsdp", axis=0, tiled=True),
        lax.all_gather(down_bias, "fsdp", axis=0, tiled=True),
        lax.all_gather(ln1_gain, "fsdp", axis=0, tiled=True),
        lax.all_gather(ln1_bias, "fsdp", axis=0, tiled=True),
        lax.all_gather(ln2_gain, "fsdp", axis=0, tiled=True),
        lax.all_gather(ln2_bias, "fsdp", axis=0, tiled=True),
    )
    (
        qkv_full,
        qv_full,
        out_full,
        outb_full,
        up_full,
        upb_full,
        down_full,
        downb_full,
        gain_one,
        shift_one,
        gain_two,
        shift_two,
    ) = gathered
    seq_count, local_len, features = tokens.shape
    row_count = seq_count * local_len
    total_len = local_len * lax.axis_size("fsdp")
    offset = lax.axis_index("fsdp") * local_len
    head_count = features // HD
    scale = HD ** (-0.5)
    inputs = tokens.reshape(row_count, features).astype(jnp.float32)
    normal_one, pull_one = jax.vjp(normalize, inputs)
    first = (normal_one * gain_one.astype(jnp.float32) + shift_one.astype(jnp.float32)).astype(
        jnp.bfloat16
    )
    qv_wide = qv_full.astype(jnp.float32)
    zero_keys = jnp.zeros((features,), jnp.float32)
    full_bias = jnp.concatenate([qv_wide[:features], zero_keys, qv_wide[features:]])
    mixed = (jnp.dot(first, qkv_full, preferred_element_type=jnp.float32) + full_bias).astype(
        jnp.bfloat16
    )
    queries = mixed[:, :features].reshape(seq_count, local_len, features)
    keys = mixed[:, features : 2 * features].reshape(seq_count, local_len, features)
    values = mixed[:, 2 * features :].reshape(seq_count, local_len, features)
    keys_all, values_all = (
        lax.all_gather(keys, "fsdp", axis=1, tiled=True),
        lax.all_gather(values, "fsdp", axis=1, tiled=True),
    )
    query_pos = offset + jnp.arange(local_len, dtype=jnp.int32)
    key_pos = jnp.arange(total_len, dtype=jnp.int32)
    allowed = key_pos[None, :] <= query_pos[:, None]

    def head_parts(head_index, source):
        column = head_index * HD
        return lax.dynamic_slice_in_dim(source, column, HD, 2)

    def head_scores(query_part, key_part):
        scores = (
            jnp.einsum("sqd,skd->sqk", query_part, key_part, preferred_element_type=jnp.float32)
            * scale
        )
        return jnp.where(allowed[None], scores, -1e30)

    def head_forward(head_index):
        query_part = head_parts(head_index, queries)
        key_part = head_parts(head_index, keys_all)
        value_part = head_parts(head_index, values_all)
        scores = head_scores(query_part, key_part)
        row_peak = jnp.max(scores, axis=-1, keepdims=True)
        weights = jnp.exp(scores - row_peak)
        row_total = jnp.sum(weights, axis=-1, keepdims=True)
        probabilities = (weights / row_total).astype(jnp.bfloat16)
        head_out = jnp.einsum(
            "sqk,skd->sqd", probabilities, value_part, preferred_element_type=jnp.float32
        )
        return (head_out, (row_peak + jnp.log(row_total))[..., 0])

    head_indices = jnp.arange(head_count, dtype=jnp.int32)
    per_head, logsum = lax.map(head_forward, head_indices)
    attended = per_head.transpose(1, 2, 0, 3).reshape(row_count, features).astype(jnp.bfloat16)
    branch = jnp.dot(attended, out_full, preferred_element_type=jnp.float32) + outb_full.astype(
        jnp.float32
    )
    hidden = inputs + branch
    normal_two, pull_two = jax.vjp(normalize, hidden)
    second = (normal_two * gain_two.astype(jnp.float32) + shift_two.astype(jnp.float32)).astype(
        jnp.bfloat16
    )
    upward = jnp.dot(second, up_full, preferred_element_type=jnp.float32) + upb_full.astype(
        jnp.float32
    )
    activated, pull_gelu = jax.vjp(gelu_exact, upward)
    act_low = activated.astype(jnp.bfloat16)
    result = hidden + (
        jnp.dot(act_low, down_full, preferred_element_type=jnp.float32)
        + downb_full.astype(jnp.float32)
    )
    qkv_back, out_back, up_back, down_back, gain_one_back, gain_two_back = (
        qkv_full,
        out_full,
        up_full,
        down_full,
        gain_one,
        gain_two,
    )
    upstream = cotangent.reshape(row_count, features).astype(jnp.float32)
    down_grad = cotangent.reshape(row_count, features)
    grad_down_w = jnp.einsum("rf,rd->fd", act_low, down_grad, preferred_element_type=jnp.float32)
    grad_down_b = jnp.sum(upstream, axis=0)
    grad_act = jnp.einsum("rd,fd->rf", down_grad, down_back, preferred_element_type=jnp.float32)
    (grad_upward,) = pull_gelu(grad_act)
    up_low = grad_upward.astype(jnp.bfloat16)
    grad_up_w = jnp.einsum("rd,rf->df", second, up_low, preferred_element_type=jnp.float32)
    grad_up_b = jnp.sum(up_low.astype(jnp.float32), axis=0)
    grad_second = jnp.einsum("rf,df->rd", up_low, up_back, preferred_element_type=jnp.float32)
    grad_gain_two = jnp.sum(grad_second * normal_two, axis=0)
    grad_shift_two = jnp.sum(grad_second, axis=0)
    (grad_norm_two,) = pull_two(grad_second * gain_two_back.astype(jnp.float32))
    grad_hidden = upstream + grad_norm_two
    branch_grad = grad_hidden.astype(jnp.bfloat16)
    grad_out_w = jnp.einsum("rc,rd->cd", attended, branch_grad, preferred_element_type=jnp.float32)
    grad_out_b = jnp.sum(branch_grad.astype(jnp.float32), axis=0)
    grad_att = jnp.einsum("rd,cd->rc", branch_grad, out_back, preferred_element_type=jnp.float32)
    grad_att = grad_att.astype(jnp.bfloat16).reshape(seq_count, local_len, features)

    def head_backward(head_pair):
        head_index, head_logsum = head_pair
        query_part = head_parts(head_index, queries)
        key_part = head_parts(head_index, keys_all)
        value_part = head_parts(head_index, values_all)
        grad_part = head_parts(head_index, grad_att)
        scores = head_scores(query_part, key_part)
        probabilities = jnp.exp(scores - head_logsum[..., None])
        grad_probs = jnp.einsum(
            "sqd,skd->sqk", grad_part, value_part, preferred_element_type=jnp.float32
        )
        inner_sum = jnp.sum(probabilities * grad_probs, axis=-1, keepdims=True)
        grad_scores = (probabilities * (grad_probs - inner_sum)).astype(jnp.bfloat16)
        grad_query = (
            jnp.einsum("sqk,skd->sqd", grad_scores, key_part, preferred_element_type=jnp.float32)
            * scale
        )
        grad_key = (
            jnp.einsum("sqk,sqd->skd", grad_scores, query_part, preferred_element_type=jnp.float32)
            * scale
        )
        grad_value = jnp.einsum(
            "sqk,sqd->skd",
            probabilities.astype(jnp.bfloat16),
            grad_part,
            preferred_element_type=jnp.float32,
        )
        return (grad_query, grad_key, grad_value)

    query_grads, key_grads, value_grads = lax.map(head_backward, (head_indices, logsum))
    query_grads = query_grads.transpose(1, 2, 0, 3).reshape(seq_count, local_len, features)
    key_grads = key_grads.transpose(1, 2, 0, 3).reshape(seq_count, total_len, features)
    value_grads = value_grads.transpose(1, 2, 0, 3).reshape(seq_count, total_len, features)
    own_keys, own_values = (
        lax.psum_scatter(key_grads, "fsdp", scatter_dimension=1, tiled=True),
        lax.psum_scatter(value_grads, "fsdp", scatter_dimension=1, tiled=True),
    )
    mixed_grad = jnp.concatenate([query_grads, own_keys, own_values], axis=-1)
    mixed_grad = mixed_grad.reshape(row_count, 3 * features).astype(jnp.bfloat16)
    grad_qkv_w = jnp.einsum("rd,re->de", first, mixed_grad, preferred_element_type=jnp.float32)
    column_sums = jnp.sum(mixed_grad.astype(jnp.float32), axis=0)
    grad_qv_b = jnp.concatenate([column_sums[:features], column_sums[2 * features :]])
    grad_first = jnp.einsum("re,de->rd", mixed_grad, qkv_back, preferred_element_type=jnp.float32)
    grad_gain_one = jnp.sum(grad_first * normal_one, axis=0)
    grad_shift_one = jnp.sum(grad_first, axis=0)
    (grad_norm_one,) = pull_one(grad_first * gain_one_back.astype(jnp.float32))
    grad_inputs = grad_hidden + grad_norm_one
    owned = (
        lax.psum_scatter(grad_qkv_w, "fsdp", scatter_dimension=0, tiled=True),
        lax.psum_scatter(grad_qv_b, "fsdp", scatter_dimension=0, tiled=True),
        lax.psum_scatter(grad_out_w, "fsdp", scatter_dimension=0, tiled=True),
        lax.psum_scatter(grad_out_b, "fsdp", scatter_dimension=0, tiled=True),
        lax.psum_scatter(grad_up_w, "fsdp", scatter_dimension=0, tiled=True),
        lax.psum_scatter(grad_up_b, "fsdp", scatter_dimension=0, tiled=True),
        lax.psum_scatter(grad_down_w, "fsdp", scatter_dimension=0, tiled=True),
        lax.psum_scatter(grad_down_b, "fsdp", scatter_dimension=0, tiled=True),
        lax.psum_scatter(grad_gain_one, "fsdp", scatter_dimension=0, tiled=True),
        lax.psum_scatter(grad_shift_one, "fsdp", scatter_dimension=0, tiled=True),
        lax.psum_scatter(grad_gain_two, "fsdp", scatter_dimension=0, tiled=True),
        lax.psum_scatter(grad_shift_two, "fsdp", scatter_dimension=0, tiled=True),
    )
    summed = lax.psum(
        (
            owned[0],
            owned[1],
            owned[2],
            owned[3],
            owned[4],
            owned[5],
            owned[6],
            owned[7],
            owned[8],
            owned[9],
            owned[10],
            owned[11],
        ),
        "rep",
    )
    return (
        result.reshape(seq_count, local_len, features),
        grad_inputs.reshape(seq_count, local_len, features),
        summed[0],
        summed[1],
        summed[2],
        summed[3],
        summed[4],
        summed[5],
        summed[6],
        summed[7],
        summed[8],
        summed[9],
        summed[10],
        summed[11],
    )


def solution(mesh):
    return jax.shard_map(
        local,
        mesh=mesh,
        in_specs=(
            P("rep", "fsdp", None),
            P("fsdp", None),
            P("fsdp"),
            P("fsdp", None),
            P("fsdp"),
            P("fsdp", None),
            P("fsdp"),
            P("fsdp", None),
            P("fsdp"),
            P("fsdp"),
            P("fsdp"),
            P("fsdp"),
            P("fsdp"),
            P("rep", "fsdp", None),
        ),
        out_specs=(
            P("rep", "fsdp", None),
            P("rep", "fsdp", None),
            P("fsdp", None),
            P("fsdp"),
            P("fsdp", None),
            P("fsdp"),
            P("fsdp", None),
            P("fsdp"),
            P("fsdp", None),
            P("fsdp"),
            P("fsdp"),
            P("fsdp"),
            P("fsdp"),
            P("fsdp"),
        ),
        check_vma=False,
    )
```

profile of v0, /device:TPU:0, one launch (start us, length us, event | category | flops | bytes accessed | tf_op | source)
XLA Modules:
  0.0 2490.9 jit_solution(7416294959069396741)
XLA Ops:
  18.3 29.2 %all-reduce.19 = (bf16[2176]{0:T(1024)(128)(2,1)S(1)}, bf16[1088]{0:T(1024)(128)(2,1)S(1)}, bf16[1088]{0:T(1024)(128)(2,1)S(1)}, bf16[1088]{0:T(1024)(128)(2,1)S...) all-reduce(bf16[2176]{0:T(1024)(128)(2,1)S(1)} %dynamic-update-slic, ...), channel_id=1, replica_groups=mesh['rep'=8,'fsdp'=4] {'fsdp'}, use_global_device_ids=true, to_apply=%add.2 | all-reduce | flops 13056 | bytes 52224
  50.1 94.3 %all-gather.9.cloned.1.call-done = bf16[1088,3264]{1,0:T(8,128)(2,1)} async-done(((bf16[272,3264]{1,0:T(8,128)(2,1)}), bf16[1088,3264]{1,0:T(8,128)(2,1)}) %all-gather.9.cloned.1.call-update) | async-done | bytes 7102480 | tf_op jit(solution)/shard_map/all_gather | solution.py:39
  157.6 80.0 %all-gather.17.cloned.1.call-done = bf16[2048,1088]{0,1:T(8,128)(2,1)} async-done(((bf16[512,1088]{0,1:T(8,128)(2,1)}), bf16[2048,1088]{0,1:T(8,128)(2,1)}) %all-gather.17.cloned.1.call-update) | async-done | bytes 4456464 | tf_op jit(solution)/shard_map/all_gather | solution.py:87
  244.1 79.3 %all-gather.19.cloned.1.call-done = bf16[2048,1088]{0,1:T(8,128)(2,1)} async-done(((bf16[512,1088]{0,1:T(8,128)(2,1)}), bf16[2048,1088]{0,1:T(8,128)(2,1)}) %all-gather.19.cloned.1.call-update) | async-done | bytes 4456464 | tf_op jit(solution)/shard_map/all_gather | solution.py:88
  329.9 107.8 %while.28 = (s32[]{:T(128)}, bf16[17,1,512,64]{2,3,1,0:T(8,128)(2,1)S(1)}, f32[17,1,512]{2,1,0:T(1,128)S(1)}, s32[17]{0:T(128)S(1)}, bf16[1,512,1088]{2,1,0:T(8,...) while((s32[]{:T(128)}, ...), condition=%wide.region_5.6_spmd.clone, body=%wide.region_2.5_spmd.clone.sunk | while | flops 277872128 | bytes 13917879 | solution.py:120
  443.3 100.3 %all-gather.13.cloned.1.call-done = bf16[1088,4352]{1,0:T(8,128)(2,1)} async-done(((bf16[272,4352]{1,0:T(8,128)(2,1)}), bf16[1088,4352]{1,0:T(8,128)(2,1)}) %all-gather.13.cloned.1.call-update) | async-done | bytes 9469968 | tf_op jit(solution)/shard_map/all_gather | solution.py:43
  543.5 32.4 %multiply_convert_fusion.1 = (bf16[512,4352]{1,0:T(8,128)(2,1)}, f32[512,4352]{1,0:T(8,128)}, f32[512,4352]{1,0:T(8,128)}) fusion(f32[4352]{0:T(1024)S(1)} %convert_element_type.114, bf16[1088,4352]{1,0:T(8,128)(2,1)} %all-gather.13.cloned.1.call-done, f32[512,1088]{0,1:T(8,128)S(1)} %get-tuple-element.298, f32[1088]{0:T(1024)S(1)} %convert_element_type.112, ...), kind=kOutput, calls=%fused_computation.58 | convolution fusion | flops 4998463488 | bytes 34010624 | tf_op jit(solution)/shard_map/dot_general | solution.py:130
  575.9 143.6 %all-gather.15.cloned.1.call-done = bf16[4352,1088]{1,0:T(8,128)(2,1)} async-done(((bf16[1088,1088]{1,0:T(8,128)(2,1)}), bf16[4352,1088]{1,0:T(8,128)(2,1)}) %all-gather.15.cloned.1.call-update) | async-done | bytes 9469968 | tf_op jit(solution)/shard_map/all_gather | solution.py:45
  719.6 14.6 convert_reduce_fusion
  734.2 10.8 multiply_reduce_fusion.1
  752.2 218.5 %while.29 = (s32[]{:T(128)}, bf16[17,1,512,64]{2,3,1,0:T(8,128)(2,1)S(1)}, f32[17,1,2048,64]{2,3,1,0:T(8,128)}, f32[17,1,2048,64]{2,3,1,0:T(8,128)}, s32[17]{0:T...) while((s32[]{:T(128)}, ...), condition=%wide.region_12.13_spmd.clone, body=%wide.region_10.12_spmd.clone.sunk | while | flops 681737728 | bytes 34619096 | solution.py:196
  978.2 11.9 fusion.98
  991.4 13.1 fusion.79
  1004.7 117.3 %reduce-scatter.7.cloned.1.call-done = f32[1,512,1088]{1,2,0:T(8,128)} async-done(((f32[1,2048,1088]{1,2,0:T(8,128)}), f32[1,512,1088]{1,2,0:T(8,128)}) %reduce-scatter.7.cloned.1.call-update) | async-done | bytes 2228240 | tf_op jit(solution)/shard_map/reduce_scatter | solution.py:201
  1124.8 153.3 %reduce-scatter.9.cloned.1.call-done = f32[1,512,1088]{1,2,0:T(8,128)} async-done(((f32[1,2048,1088]{1,2,0:T(8,128)}), f32[1,512,1088]{1,2,0:T(8,128)}) %reduce-scatter.9.cloned.1.call-update) | async-done | bytes 2228240 | tf_op jit(solution)/shard_map/reduce_scatter | solution.py:202
  1280.4 10.1 fusion.50
  1290.8 81.1 %reduce-scatter.13.cloned.1.call-done = f32[272,1088]{1,0:T(8,128)} async-done(((f32[1088,1088]{1,0:T(8,128)}), f32[272,1088]{1,0:T(8,128)}) %reduce-scatter.13.cloned.1.call-update) | async-done | bytes 1183760 | tf_op jit(solution)/shard_map/reduce_scatter | solution.py:217
  1371.9 318.4 %reduce-scatter.15.cloned.1.call-done = f32[272,4352]{1,0:T(8,128)} async-done(((f32[1088,4352]{1,0:T(8,128)}), f32[272,4352]{1,0:T(8,128)}) %reduce-scatter.15.cloned.1.call-update) | async-done | bytes 4734992 | tf_op jit(solution)/shard_map/reduce_scatter | solution.py:219
  1690.3 336.1 %reduce-scatter.17.cloned.1.call-done = f32[1088,1088]{1,0:T(8,128)} async-done(((f32[4352,1088]{1,0:T(8,128)}), f32[1088,1088]{1,0:T(8,128)}) %reduce-scatter.17.cloned.1.call-update) | async-done | bytes 4734992 | tf_op jit(solution)/shard_map/reduce_scatter | solution.py:221
  2026.4 246.0 %reduce-scatter.11.cloned.1.call-done = f32[272,3264]{1,0:T(8,128)} async-done(((f32[1088,3264]{1,0:T(8,128)}), f32[272,3264]{1,0:T(8,128)}) %reduce-scatter.11.cloned.1.call-update) | async-done | bytes 3551248 | tf_op jit(solution)/shard_map/reduce_scatter | solution.py:215
  2274.4 13.9 fusion.56
  2302.7 20.0 all-reduce.18
  2323.3 24.3 all-reduce.16
  2347.5 125.3 %all-reduce.22.cloned.1.call-done = (f32[272,3264]{1,0:T(8,128)}, f32[272,1088]{1,0:T(8,128)}, f32[272,4352]{1,0:T(8,128)}, f32[1088,1088]{1,0:T(8,128)}) async-done(((f32[272,3264]{1,0:T(8,128)}, f32[272,1088]{1,0:T(8,128)}, f32[272,4352]{1,0:T(8,128)}, f32[1088,1088]{1,0:T(8,128)}), (f32[272,3264]{1,0:T(8,128)}, f32[272,1088]{1,0:T(8,128)}, f32[272,4352]{1,0:T(8,128)}, ...) | async-done | bytes 14204944 | tf_op jit(solution)/shard_map/psum | solution.py:228
  (417 shorter events, 393.3 us)
Async XLA Ops:
  7.2 137.2 %all-gather.9.cloned.1.call-start = ((), (), s32[]{:S(2)}) async-start(), calls=%async_computation.6 | async-start | bytes 9052160 | tf_op jit(solution)/shard_map/all_gather | solution.py:39
  7.9 229.8 %all-gather.17.cloned.1.call-start = ((), (), s32[]{:S(2)}) async-start(), calls=%async_computation.16 | async-start | bytes 5570560 | tf_op jit(solution)/shard_map/all_gather | solution.py:87
  47.5 104.9 %copy-start.18 = (f32[1088]{0:T(1024)}, f32[1088]{0:T(1024)S(1)}, u32[]{:S(2)}) copy-start(f32[1088]{0:T(1024)S(1)} %convert_element_type.102) | copy-start | bytes 13060
  47.5 104.9 %copy-start.27 = (f32[1088]{0:T(1024)}, f32[1088]{0:T(1024)S(1)}, u32[]{:S(2)}) copy-start(f32[1088]{0:T(1024)S(1)} %convert_element_type.103) | copy-start | bytes 13060
  49.1 103.2 %copy-start.20 = (f32[512]{0:T(512)}, f32[512]{0:T(512)S(1)}, u32[]{:S(2)}) copy-start(f32[512]{0:T(512)S(1)} %broadcast_multiply_fusion.1) | copy-start | bytes 6148
  50.1 102.3 %copy-start.25 = (f32[512]{0:T(512)}, f32[512]{0:T(512)S(1)}, u32[]{:S(2)}) copy-start(f32[512]{0:T(512)S(1)} %fusion.94) | copy-start | bytes 6148
  154.1 169.3 %all-gather.19.cloned.1.call-start = ((), (), s32[]{:S(2)}) async-start(), calls=%async_computation.17 | async-start | bytes 5570560 | tf_op jit(solution)/shard_map/all_gather | solution.py:88
  154.8 283.0 %all-gather.11.cloned.1.call-start = ((), (), s32[]{:S(2)}) async-start(), calls=%async_computation.7 | async-start | bytes 3133440 | tf_op jit(solution)/shard_map/all_gather | solution.py:41
  155.4 388.1 %all-gather.13.cloned.1.call-start = ((), (), s32[]{:S(2)}) async-start(), calls=%async_computation.8 | async-start | bytes 11837440 | tf_op jit(solution)/shard_map/all_gather | solution.py:43
  156.0 563.6 %all-gather.15.cloned.1.call-start = ((), (), s32[]{:S(2)}) async-start(), calls=%async_computation.9 | async-start | bytes 12533760 | tf_op jit(solution)/shard_map/all_gather | solution.py:45
  156.6 965.5 %reduce-scatter.7.cloned.1.call-start = ((), (), s32[]{:S(2)}) async-start(), calls=%async_computation.10 | async-start | bytes 11141120 | tf_op jit(solution)/shard_map/reduce_scatter | solution.py:201
  442.9 291.3 %copy-start.2 = (f32[512,1088]{0,1:T(8,128)}, f32[512,1088]{0,1:T(8,128)S(1)}, u32[]{:S(2)}) copy-start(f32[512,1088]{0,1:T(8,128)S(1)} %get-tuple-element.298) | copy-start | bytes 6684676
  443.2 276.3 %copy-start.9 = (bf16[1,512,1088]{1,2,0:T(8,128)(2,1)S(1)}, bf16[1,512,1088]{1,2,0:T(8,128)(2,1)}, u32[]{:S(2)}) copy-start(bf16[1,512,1088]{1,2,0:T(8,128)(2,1)} %param.31) | copy-start | bytes 3342340
  971.7 306.4 %reduce-scatter.9.cloned.1.call-start = ((), (), s32[]{:S(2)}) async-start(), calls=%async_computation.11 | async-start | bytes 11141120 | tf_op jit(solution)/shard_map/reduce_scatter | solution.py:202
  972.5 399.4 %reduce-scatter.13.cloned.1.call-start = ((), (), s32[]{:S(2)}) async-start(), calls=%async_computation.13 | async-start | bytes 6266880 | tf_op jit(solution)/shard_map/reduce_scatter | solution.py:217
  978.2 712.1 %reduce-scatter.15.cloned.1.call-start = ((), (), s32[]{:S(2)}) async-start(), calls=%async_computation.14 | async-start | bytes 23674880 | tf_op jit(solution)/shard_map/reduce_scatter | solution.py:219
  990.2 1036.3 %reduce-scatter.17.cloned.1.call-start = ((), (), s32[]{:S(2)}) async-start(), calls=%async_computation.15 | async-start | bytes 25067520 | tf_op jit(solution)/shard_map/reduce_scatter | solution.py:221
  1004.6 275.5 %copy-start.1 = (bf16[1,512,1088]{1,2,0:T(8,128)(2,1)S(1)}, bf16[1,512,1088]{1,2,0:T(8,128)(2,1)}, u32[]{:S(2)}) copy-start(bf16[1,512,1088]{1,2,0:T(8,128)(2,1)} %param.18) | copy-start | bytes 3342340
  1004.6 275.5 %copy-start.19 = (f32[1088]{0:T(1024)S(1)}, f32[1088]{0:T(1024)}, u32[]{:S(2)}) copy-start(f32[1088]{0:T(1024)} %copy-done.18) | copy-start | bytes 13060
  1004.6 275.5 %copy-start.21 = (f32[512]{0:T(512)S(1)}, f32[512]{0:T(512)}, u32[]{:S(2)}) copy-start(f32[512]{0:T(512)} %copy-done.20) | copy-start | bytes 6148
  1004.6 275.5 %copy-start.26 = (f32[512]{0:T(512)S(1)}, f32[512]{0:T(512)}, u32[]{:S(2)}) copy-start(f32[512]{0:T(512)} %copy-done.25) | copy-start | bytes 6148
  1004.6 275.5 %copy-start.28 = (f32[1088]{0:T(1024)S(1)}, f32[1088]{0:T(1024)}, u32[]{:S(2)}) copy-start(f32[1088]{0:T(1024)} %copy-done.27) | copy-start | bytes 13060
  1004.6 1267.8 %reduce-scatter.11.cloned.1.call-start = ((), (), s32[]{:S(2)}) async-start(), calls=%async_computation.12 | async-start | bytes 18104320 | tf_op jit(solution)/shard_map/reduce_scatter | solution.py:215
  1290.5 1182.3 %all-reduce.22.cloned.1.call-start = ((), (), s32[]{:S(2)}) async-start(), calls=%async_computation.18 | async-start | bytes 29245440 | tf_op jit(solution)/shard_map/psum | solution.py:228
  (25 other events, 125.6 us)
Sparse Core Ops, SparseCore 0:
  9.6 134.7 all-gather.8
  154.2 83.4 all-gather.16
  239.8 83.4 all-gather.18
  324.8 51.2 all-gather.10
  377.5 165.9 all-gather.12
  545.0 174.5 all-gather.14
  970.9 151.0 reduce-scatter.6
  1124.4 153.6 reduce-scatter.8
  1281.0 90.8 reduce-scatter.12
  1374.1 316.1 reduce-scatter.14
  1692.7 333.6 reduce-scatter.16
  2028.6 243.7 reduce-scatter.10
  2276.4 196.3 all-reduce.21
where the time goes:
time: 2500 us; the launch traced here: 2490 us
  waiting for transfers between devices  1880 us (75%)
  matrix products  397 us (16%)
  blocking collectives  73.5 us (3%)
  local copies, waits for them, and re-layouts  64.3 us (3%)
  other arithmetic  34.1 us (1%)
    reduce_scatter x1, waiting for transfers between devices, local(): lax.psum_scatter(grad_down_w, 'fsdp', scatter_dimension=0, tiled=True)  336 us
    reduce_scatter x1, waiting for transfers between devices, local(): lax.psum_scatter(grad_up_w, 'fsdp', scatter_dimension=0, tiled=True)  318 us
    reduce_scatter x1, waiting for transfers between devices, local(): lax.psum_scatter(grad_qkv_w, 'fsdp', scatter_dimension=0, tiled=True)  246 us
    reduce_scatter x1, waiting for transfers between devices, local(): lax.psum_scatter(value_grads, 'fsdp', scatter_dimension=1, tiled=True)  153 us
    all_gather x1, waiting for transfers between devices, local(): lax.all_gather(w_down, 'fsdp', axis=0, tiled=True)  144 us
    psum x1, waiting for transfers between devices, local(): lax.psum((owned[0], owned[1], owned[2], owned[3], owned[4], owned[5], own...  125 us
    reduce_scatter x1, waiting for transfers between devices, local(): lax.psum_scatter(key_grads, 'fsdp', scatter_dimension=1, tiled=True)  117 us
    all_gather x1, waiting for transfers between devices, local(): lax.all_gather(w_up, 'fsdp', axis=0, tiled=True)  100 us
  transfers between devices with their start and end apart: 13, of which 12 were waited for; matrix products, arithmetic and copies ran while one was open for 9% of the time, Pallas kernels for 0%

commit v1 on v0

--- a/solution.py
+++ b/solution.py
@@ -35,35 +35,42 @@
     ln2_bias,
     cotangent,
 ):
-    gathered = (
-        lax.all_gather(w_qkv, "fsdp", axis=0, tiled=True),
-        lax.all_gather(qv_bias, "fsdp", axis=0, tiled=True),
-        lax.all_gather(w_out, "fsdp", axis=0, tiled=True),
-        lax.all_gather(out_bias, "fsdp", axis=0, tiled=True),
-        lax.all_gather(w_up, "fsdp", axis=0, tiled=True),
-        lax.all_gather(up_bias, "fsdp", axis=0, tiled=True),
-        lax.all_gather(w_down, "fsdp", axis=0, tiled=True),
-        lax.all_gather(down_bias, "fsdp", axis=0, tiled=True),
-        lax.all_gather(ln1_gain, "fsdp", axis=0, tiled=True),
-        lax.all_gather(ln1_bias, "fsdp", axis=0, tiled=True),
-        lax.all_gather(ln2_gain, "fsdp", axis=0, tiled=True),
-        lax.all_gather(ln2_bias, "fsdp", axis=0, tiled=True),
-    )
-    (
-        qkv_full,
-        qv_full,
-        out_full,
-        outb_full,
-        up_full,
-        upb_full,
-        down_full,
-        downb_full,
-        gain_one,
-        shift_one,
-        gain_two,
-        shift_two,
-    ) = gathered
     seq_count, local_len, features = tokens.shape
+    rows = w_qkv.shape[0]
+    reps = lax.axis_size("rep")
+    rep_at = lax.axis_index("rep")
+    everyone = ("fsdp", "rep")
+
+    def own_piece(matrix):
+        part = matrix.shape[0] // reps
+        return lax.dynamic_slice_in_dim(matrix, rep_at * part, part, 0)
+
+    def to_units(matrix):
+        blocks = matrix.shape[1] // features
+        return matrix.reshape(rows, blocks, features).transpose(1, 0, 2)
+
+    def gather_all(matrix):
+        return lax.all_gather(own_piece(matrix), everyone, axis=0, tiled=True)
+
+    def from_units(units):
+        blocks = units.shape[1]
+        return units.transpose(0, 2, 1, 3).reshape(features, blocks * features)
+
+    pack_one = jnp.concatenate([to_units(w_qkv), to_units(w_out)], 0)
+    units_one = gather_all(pack_one.reshape(-1, features)).reshape(-1, 4, rows, features)
+    units_up = gather_all(to_units(w_up).reshape(-1, features)).reshape(-1, 4, rows, features)
+    down_full = gather_all(w_down)
+    qkv_full = from_units(units_one[:, :3])
+    out_full = from_units(units_one[:, 3:])
+    up_full = from_units(units_up)
+    vectors = (qv_bias, out_bias, up_bias, down_bias, ln1_gain, ln1_bias, ln2_gain, ln2_bias)
+    small = lax.all_gather(jnp.concatenate(vectors), "fsdp", axis=0)
+    pieces = []
+    start = 0
+    for vector in vectors:
+        pieces.append(small[:, start : start + vector.shape[0]].reshape(-1))
+        start += vector.shape[0]
+    qv_full, outb_full, upb_full, downb_full, gain_one, shift_one, gain_two, shift_two = pieces
     row_count = seq_count * local_len
     total_len = local_len * lax.axis_size("fsdp")
     offset = lax.axis_index("fsdp") * local_len
@@ -198,11 +205,13 @@
     key_grads = key_grads.transpose(1, 2, 0, 3).reshape(seq_count, total_len, features)
     value_grads = value_grads.transpose(1, 2, 0, 3).reshape(seq_count, total_len, features)
     own_keys, own_values = (
-        lax.psum_scatter(key_grads, "fsdp", scatter_dimension=1, tiled=True),
-        lax.psum_scatter(value_grads, "fsdp", scatter_dimension=1, tiled=True),
-    )
-    mixed_grad = jnp.concatenate([query_grads, own_keys, own_values], axis=-1)
-    mixed_grad = mixed_grad.reshape(row_count, 3 * features).astype(jnp.bfloat16)
+        lax.psum_scatter(key_grads.astype(jnp.bfloat16), "fsdp", scatter_dimension=1, tiled=True),
+        lax.psum_scatter(value_grads.astype(jnp.bfloat16), "fsdp", scatter_dimension=1, tiled=True),
+    )
+    mixed_grad = jnp.concatenate(
+        [query_grads.astype(jnp.bfloat16), own_keys, own_values], axis=-1
+    )
+    mixed_grad = mixed_grad.reshape(row_count, 3 * features)
     grad_qkv_w = jnp.einsum("rd,re->de", first, mixed_grad, preferred_element_type=jnp.float32)
     column_sums = jnp.sum(mixed_grad.astype(jnp.float32), axis=0)
     grad_qv_b = jnp.concatenate([column_sums[:features], column_sums[2 * features :]])
@@ -211,52 +220,55 @@
     grad_shift_one = jnp.sum(grad_first, axis=0)
     (grad_norm_one,) = pull_one(grad_first * gain_one_back.astype(jnp.float32))
     grad_inputs = grad_hidden + grad_norm_one
-    owned = (
-        lax.psum_scatter(grad_qkv_w, "fsdp", scatter_dimension=0, tiled=True),
-        lax.psum_scatter(grad_qv_b, "fsdp", scatter_dimension=0, tiled=True),
-        lax.psum_scatter(grad_out_w, "fsdp", scatter_dimension=0, tiled=True),
-        lax.psum_scatter(grad_out_b, "fsdp", scatter_dimension=0, tiled=True),
-        lax.psum_scatter(grad_up_w, "fsdp", scatter_dimension=0, tiled=True),
-        lax.psum_scatter(grad_up_b, "fsdp", scatter_dimension=0, tiled=True),
-        lax.psum_scatter(grad_down_w, "fsdp", scatter_dimension=0, tiled=True),
-        lax.psum_scatter(grad_down_b, "fsdp", scatter_dimension=0, tiled=True),
-        lax.psum_scatter(grad_gain_one, "fsdp", scatter_dimension=0, tiled=True),
-        lax.psum_scatter(grad_shift_one, "fsdp", scatter_dimension=0, tiled=True),
-        lax.psum_scatter(grad_gain_two, "fsdp", scatter_dimension=0, tiled=True),
-        lax.psum_scatter(grad_shift_two, "fsdp", scatter_dimension=0, tiled=True),
-    )
-    summed = lax.psum(
-        (
-            owned[0],
-            owned[1],
-            owned[2],
-            owned[3],
-            owned[4],
-            owned[5],
-            owned[6],
-            owned[7],
-            owned[8],
-            owned[9],
-            owned[10],
-            owned[11],
-        ),
-        "rep",
-    )
+    fsdp = lax.axis_size("fsdp")
+
+    def grad_units(matrix):
+        blocks = matrix.shape[1] // features
+        return matrix.astype(jnp.bfloat16).reshape(fsdp, rows, blocks, features).transpose(0, 2, 1, 3)
+
+    def reduce_all(matrix):
+        part = lax.psum_scatter(matrix, everyone, scatter_dimension=0, tiled=True)
+        return lax.all_gather(part, "rep", axis=0, tiled=True)
+
+    def own_matrix(units):
+        blocks = units.shape[0] // rows
+        wide = units.reshape(blocks, rows, features).transpose(1, 0, 2)
+        return wide.reshape(rows, blocks * features).astype(jnp.float32)
+
+    down_own = reduce_all(grad_down_w.astype(jnp.bfloat16)).astype(jnp.float32)
+    up_own = own_matrix(reduce_all(grad_units(grad_up_w).reshape(-1, features)))
+    packed = jnp.concatenate([grad_units(grad_qkv_w), grad_units(grad_out_w)], 1)
+    one_own = reduce_all(packed.reshape(-1, features))
+    qkv_own = own_matrix(one_own[: 3 * rows])
+    out_own = own_matrix(one_own[3 * rows :])
+    small_grads = (
+        grad_qv_b, grad_out_b, grad_up_b, grad_down_b,
+        grad_gain_one, grad_shift_one, grad_gain_two, grad_shift_two,
+    )
+    stacked = jnp.concatenate([g.reshape(fsdp, -1) for g in small_grads], 1)
+    stacked = lax.psum(stacked, ("rep", "fsdp"))
+    mine = lax.dynamic_index_in_dim(stacked, lax.axis_index("fsdp"), 0, keepdims=False)
+    small_own = []
+    start = 0
+    for g in small_grads:
+        width = g.shape[0] // fsdp
+        small_own.append(mine[start : start + width])
+        start += width
     return (
         result.reshape(seq_count, local_len, features),
         grad_inputs.reshape(seq_count, local_len, features),
-        summed[0],
-        summed[1],
-        summed[2],
-        summed[3],
-        summed[4],
-        summed[5],
-        summed[6],
-        summed[7],
-        summed[8],
-        summed[9],
-        summed[10],
-        summed[11],
+        qkv_own,
+        small_own[0],
+        out_own,
+        small_own[1],
+        up_own,
+        small_own[2],
+        down_own,
+        small_own[3],
+        small_own[4],
+        small_own[5],
+        small_own[6],
+        small_own[7],
     )
 
 

time: 2500 us -> 1500 us (0.60)
  waiting for transfers between devices: 1880 us -> 692 us
  local copies, waits for them, and re-layouts: 64.3 us -> 220 us
    reduce_scatter x6 -> x2, waiting for transfers between devices: 1250 us -> 97.7 us  [the longest x1 83.9 us: local(): lax.psum_scatter(value_grads.astype(jnp.bfloat16), 'fsdp', scatter_dimens...]
    unnamed x13 -> x16, waiting for transfers between devices: 3.78 us -> 366 us
    all_gather x4 -> x6, waiting for transfers between devices: 338 us -> 90.3 us  [the longest x3 86.1 us: gather_all(): return lax.all_gather(own_piece(matrix), everyone, axis=0, tiled=True)]
    psum x1 -> x0, waiting for transfers between devices: 125 us -> none  [local(): lax.psum((owned[0], owned[1], owned[2], owned[3], owned[4], owned[5], own...]
    reshape x0 -> x15, local copies, waits for them, and re-layouts: none -> 106 us  [the longest x3 47.3 us: grad_units(): matrix.astype(jnp.bfloat16).reshape(fsdp, rows, blocks, features)]
    unnamed x2 -> x1, blocking collectives: 49.2 us -> 21.6 us
  transfers between devices with their start and end apart: 13 -> 13, of which waited for: 12 -> 10; matrix products, arithmetic and copies ran while one was open for 9% -> 28% of each run, Pallas kernels for 0% -> 0%
where the time goes in v1:
time: 1500 us; the launch traced here: 1480 us
  waiting for transfers between devices  692 us (46%)
  matrix products  414 us (28%)
  local copies, waits for them, and re-layouts  220 us (15%)
  blocking collectives  61.8 us (4%)
  other arithmetic  57.4 us (4%)
  loops' own time  23 us (2%)
  between operations  15.4 us (1%)
    unnamed x16, waiting for transfers between devices  366 us
    all_gather x3, waiting for transfers between devices, gather_all(): return lax.all_gather(own_piece(matrix), everyone, axis=0, tiled=True)  86.1 us
    reduce_scatter x1, waiting for transfers between devices, local(): lax.psum_scatter(value_grads.astype(jnp.bfloat16), 'fsdp', scatter_dimens...  83.9 us
    dot_general x34, matrix products, head_scores(): jnp.einsum('sqd,skd->sqk', query_part, key_part, preferred_element_type=j...  83.4 us
    all_gather x1, waiting for transfers between devices, local(): lax.all_gather(values, 'fsdp', axis=1, tiled=True)  79.1 us
    all_gather x1, waiting for transfers between devices, local(): lax.all_gather(keys, 'fsdp', axis=1, tiled=True)  59.5 us
    dot_general x17, matrix products, head_forward(): jnp.einsum('sqk,skd->sqd', probabilities, value_part, preferred_element_t...  48.9 us
    reshape x3, local copies, waits for them, and re-layouts, grad_units(): matrix.astype(jnp.bfloat16).reshape(fsdp, rows, blocks, features)  47.3 us
  transfers between devices with their start and end apart: 13, of which 10 were waited for; matrix products, arithmetic and copies ran while one was open for 28% of the time, Pallas kernels for 0%

profile of v1, /device:TPU:0, one launch (start us, length us, event | category | flops | bytes accessed | tf_op | source)
XLA Modules:
  0.0 1484.9 jit_solution(5618912969653301980)
XLA Ops:
  33.1 21.6 %all-reduce = bf16[13056]{0:T(1024)(128)(2,1)S(1)} all-reduce(bf16[13056]{0:T(1024)(128)(2,1)S(1)} %dynamic-update-slice), channel_id=2, replica_groups=mesh['rep'=8,'fsdp'=4] {'fsdp'}, use_global_device_ids=true, to_apply=%add | all-reduce | flops 13056 | bytes 52224
  59.0 50.1 %all-gather.12.cloned.1.call-done = bf16[4352,1088]{1,0:T(8,128)(2,1)} async-done(((bf16[136,1088]{1,0:T(8,128)(2,1)}), bf16[4352,1088]{1,0:T(8,128)(2,1)}) %all-gather.12.cloned.1.call-update) | async-done | bytes 9469968 | tf_op jit(solution)/shard_map/all_gather | solution.py:53
  112.8 10.9 copy.91
  123.7 19.2 %reshape.472 = bf16[1088,3264]{1,0:T(8,128)(2,1)} reshape(bf16[4,272,3,1088]{3,2,1,0:T(4,128)(2,1)} %bitcast.241) | data formatting | bytes 14204928 | tf_op jit(solution)/shard_map/reshape | solution.py:57
  159.2 36.0 %all-gather.14.cloned.1.call-done = bf16[4352,1088]{1,0:T(8,128)(2,1)} async-done(((bf16[136,1088]{1,0:T(8,128)(2,1)}), bf16[4352,1088]{1,0:T(8,128)(2,1)}) %all-gather.14.cloned.1.call-update) | async-done | bytes 9469968 | tf_op jit(solution)/shard_map/all_gather | solution.py:53
  204.9 16.7 %reshape.479 = bf16[1088,4352]{1,0:T(8,128)(2,1)} reshape(bf16[4,272,4,1088]{3,2,1,0:T(4,128)(2,1)} %bitcast.240) | data formatting | bytes 18939904 | tf_op jit(solution)/shard_map/reshape | solution.py:57
  221.6 59.5 %all-gather.24.cloned.1.call-done = bf16[2048,1088]{0,1:T(8,128)(2,1)} async-done(((bf16[512,1088]{0,1:T(8,128)(2,1)}), bf16[2048,1088]{0,1:T(8,128)(2,1)}) %all-gather.24.cloned.1.call-update) | async-done | bytes 4456464 | tf_op jit(solution)/shard_map/all_gather | solution.py:94
  287.4 79.1 %all-gather.26.cloned.1.call-done = bf16[2048,1088]{0,1:T(8,128)(2,1)} async-done(((bf16[512,1088]{0,1:T(8,128)(2,1)}), bf16[2048,1088]{0,1:T(8,128)(2,1)}) %all-gather.26.cloned.1.call-update) | async-done | bytes 4456464 | tf_op jit(solution)/shard_map/all_gather | solution.py:95
  374.1 118.2 %while.28 = (s32[]{:T(128)}, bf16[17,1,512,64]{2,3,1,0:T(8,128)(2,1)}, f32[17,1,512]{2,1,0:T(1,128)S(1)}, s32[17]{0:T(128)S(1)}, bf16[1,512,1088]{2,1,0:T(8,128)...) while((s32[]{:T(128)}, ...), condition=%wide.region_5.6_spmd.clone, body=%wide.region_2.5_spmd.clone.sunk | while | flops 277872128 | bytes 13917879 | solution.py:127
  497.9 32.6 %multiply_convert_fusion.1 = (bf16[512,4352]{1,0:T(8,128)(2,1)}, f32[512,4352]{1,0:T(8,128)}, f32[512,4352]{1,0:T(8,128)}) fusion(f32[4352]{0:T(1024)S(1)} %reshape.501, bf16[1088,4352]{1,0:T(8,128)(2,1)} %reshape.479, f32[512,1088]{0,1:T(8,128)S(1)} %get-tuple-element.318, f32[1088]{0:T(1024)S(1)} %reshape.500, f32[1088]{0:T(1024)S(1)} %reshape.499, ...), kind=kOutput, calls=%fused_computation.72 | convolution fusion | flops 4998463488 | bytes 34010624 | tf_op jit(solution)/shard_map/dot_general | solution.py:137
  530.5 18.5 %convert_reduce_fusion = (f32[4352]{0:T(1024)}, bf16[512,4352]{1,0:T(8,128)(2,1)}) fusion(f32[512,4352]{1,0:T(8,128)} %get-tuple-element.297, bf16[4352,1088]{1,0:T(8,128)(2,1)} %all-gather.16.cloned.1.call-done, bf16[1,512,1088]{1,2,0:T(8,128)(2,1)S(1)} %copy-done.12, f32[512,4352]{1,0:T(8,128)} %get-tuple-element.319, f32[4352]{0:T(1024)S(1)} %reshape.501), kind=kOutput, calls=%fused_computation.71 | convolution fusion | flops 4886491136 | bytes 32901120 | tf_op jit(solution)/shard_map/rd,fd->rf/dot_general | solution.py:158
  566.5 225.4 %while.29 = (s32[]{:T(128)}, bf16[17,1,512,64]{2,3,1,0:T(8,128)(2,1)}, bf16[17,1,2048,64]{2,3,1,0:T(8,128)(2,1)}, bf16[17,1,2048,64]{2,3,1,0:T(8,128)(2,1)}, s32...) while((s32[]{:T(128)}, ...), condition=%wide.region_12.13_spmd.clone, body=%wide.region_10.12_spmd.clone.sunk | while | flops 681737728 | bytes 34619096 | solution.py:203
  793.6 10.0 convolution_convert_fusion.1
  803.6 18.7 %reshape.494 = bf16[4,272,4,1088]{3,2,1,0:T(4,128)(2,1)} reshape(bf16[1088,4352]{1,0:T(8,128)(2,1)} %convolution_convert_fusion.1) | data formatting | bytes 18939904 | tf_op jit(solution)/shard_map/reshape | solution.py:227
  832.4 11.8 convolution_convert_fusion
  857.8 13.8 reduce-scatter.12.cloned.1.call-done
  871.6 83.9 %reduce-scatter.14.cloned.1.call-done = bf16[1,512,1088]{1,2,0:T(8,128)(2,1)} async-done(((bf16[1,2048,1088]{1,2,0:T(8,128)(2,1)}), bf16[1,512,1088]{1,2,0:T(8,128)(2,1)}) %reduce-scatter.14.cloned.1.call-update) | async-done | bytes 1114128 | tf_op jit(solution)/shard_map/reduce_scatter | solution.py:209
  963.8 19.8 %reshape.485 = bf16[4,272,3,1088]{3,2,1,0:T(4,128)(2,1)} reshape(bf16[1088,3264]{1,0:T(8,128)(2,1)} %convolution_convert_fusion.2) | data formatting | bytes 14204928 | tf_op jit(solution)/shard_map/reshape | solution.py:227
  983.5 13.9 pad_maximum_fusion
  1006.5 88.7 %reduce-scatter.18.cloned.1.call-done = bf16[136,1088]{1,0:T(8,128)(2,1)} async-done(((bf16[4352,1088]{1,0:T(8,128)(2,1)}), bf16[136,1088]{1,0:T(8,128)(2,1)}) %reduce-scatter.18.cloned.1.call-update) | async-done | bytes 295952
  1095.3 138.1 %reduce-scatter.20.cloned.1.call-done = bf16[136,1088]{1,0:T(8,128)(2,1)} async-done(((bf16[4352,1088]{1,0:T(8,128)(2,1)}), bf16[136,1088]{1,0:T(8,128)(2,1)}) %reduce-scatter.20.cloned.1.call-update) | async-done | bytes 295952
  1233.9 137.5 %reduce-scatter.16.cloned.1.call-done = bf16[136,1088]{1,0:T(8,128)(2,1)} async-done(((bf16[4352,1088]{1,0:T(8,128)(2,1)}), bf16[136,1088]{1,0:T(8,128)(2,1)}) %reduce-scatter.16.cloned.1.call-update) | async-done | bytes 295952
  1371.4 13.9 fusion.57
  1401.1 40.2 %psum.7 = f32[4,3264]{1,0:T(4,128)S(1)} all-reduce(f32[4,3264]{1,0:T(4,128)S(1)} %concatenate.34), channel_id=1, replica_groups=mesh['rep'=8,'fsdp'=4] {'rep','fsdp'}, use_global_device_ids=true, to_apply=%region_26.27 | all-reduce | flops 13056 | bytes 104448 | tf_op jit(solution)/shard_map/psum | solution.py:249
  (450 shorter events, 512.3 us)
Async XLA Ops:
  7.2 146.6 %copy-start = (bf16[1088,1088]{1,0:T(8,128)(2,1)S(1)}, bf16[1088,1088]{1,0:T(8,128)(2,1)}, u32[]{:S(2)}) copy-start(bf16[1088,1088]{1,0:T(8,128)(2,1)} %param.25) | copy-start | bytes 7102468
  7.2 101.9 %all-gather.12.cloned.1.call-start = ((), (), s32[]{:S(2)}) async-start(), calls=%async_computation.5 | async-start | bytes 10340352 | tf_op jit(solution)/shard_map/all_gather | solution.py:53
  22.0 173.2 %all-gather.14.cloned.1.call-start = ((), (), s32[]{:S(2)}) async-start(), calls=%async_computation.6 | async-start | bytes 10340352 | tf_op jit(solution)/shard_map/all_gather | solution.py:53
  31.3 249.7 %all-gather.24.cloned.1.call-start = ((), (), s32[]{:S(2)}) async-start(), calls=%async_computation.13 | async-start | bytes 5570560 | tf_op jit(solution)/shard_map/all_gather | solution.py:94
  55.5 87.4 %copy-start.21 = (f32[1088]{0:T(1024)}, f32[1088]{0:T(1024)S(1)}, u32[]{:S(2)}) copy-start(f32[1088]{0:T(1024)S(1)} %reshape.496) | copy-start | bytes 13060
  55.8 87.1 %copy-start.33 = (f32[1088]{0:T(1024)}, f32[1088]{0:T(1024)S(1)}, u32[]{:S(2)}) copy-start(f32[1088]{0:T(1024)S(1)} %reshape.497) | copy-start | bytes 13060
  57.4 85.6 %copy-start.23 = (f32[512]{0:T(512)}, f32[512]{0:T(512)S(1)}, u32[]{:S(2)}) copy-start(f32[512]{0:T(512)S(1)} %broadcast_multiply_fusion.1) | copy-start | bytes 6148
  153.1 213.4 %all-gather.26.cloned.1.call-start = ((), (), s32[]{:S(2)}) async-start(), calls=%async_computation.14 | async-start | bytes 5570560 | tf_op jit(solution)/shard_map/all_gather | solution.py:95
  153.7 376.8 %all-gather.16.cloned.1.call-start = ((), (), s32[]{:S(2)}) async-start(), calls=%async_computation.7 | async-start | bytes 10340352 | tf_op jit(solution)/shard_map/all_gather | solution.py:53
  154.5 717.0 %reduce-scatter.12.cloned.1.call-start = ((), (), s32[]{:S(2)}) async-start(), calls=%async_computation.8 | async-start | bytes 5570560 | tf_op jit(solution)/shard_map/reduce_scatter | solution.py:208
  374.1 118.2 %copy-start.4 = (bf16[1,512,1088]{1,2,0:T(8,128)(2,1)S(1)}, bf16[1,512,1088]{1,2,0:T(8,128)(2,1)}, u32[]{:S(2)}) copy-start(bf16[1,512,1088]{1,2,0:T(8,128)(2,1)} %param.18) | copy-start | bytes 3342340
  791.9 163.5 %reduce-scatter.14.cloned.1.call-start = ((), (), s32[]{:S(2)}) async-start(), calls=%async_computation.9 | async-start | bytes 5570560 | tf_op jit(solution)/shard_map/reduce_scatter | solution.py:209
  792.7 302.5 %reduce-scatter.18.cloned.1.call-start = ((), (), s32[]{:S(2)}) async-start(), calls=%async_computation.16 | async-start | bytes 10340352
  831.2 402.2 %reduce-scatter.20.cloned.1.call-start = ((), (), s32[]{:S(2)}) async-start(), calls=%async_computation.17 | async-start | bytes 10340352
  844.2 527.2 %reduce-scatter.16.cloned.1.call-start = ((), (), s32[]{:S(2)}) async-start(), calls=%async_computation.15 | async-start | bytes 10340352
  849.8 105.6 %copy-start.5 = (bf16[1,512,1088]{1,2,0:T(8,128)(2,1)S(1)}, bf16[1,512,1088]{1,2,0:T(8,128)(2,1)}, u32[]{:S(2)}) copy-start(bf16[1,512,1088]{1,2,0:T(8,128)(2,1)} %param.18) | copy-start | bytes 3342340
  849.8 105.6 %copy-start.22 = (f32[1088]{0:T(1024)S(1)}, f32[1088]{0:T(1024)}, u32[]{:S(2)}) copy-start(f32[1088]{0:T(1024)} %copy-done.21) | copy-start | bytes 13060
  849.8 105.6 %copy-start.24 = (f32[512]{0:T(512)S(1)}, f32[512]{0:T(512)}, u32[]{:S(2)}) copy-start(f32[512]{0:T(512)} %copy-done.23) | copy-start | bytes 6148
  849.8 105.6 %copy-start.30 = (f32[512]{0:T(512)S(1)}, f32[512]{0:T(512)}, u32[]{:S(2)}) copy-start(f32[512]{0:T(512)} %copy-done.29) | copy-start | bytes 6148
  849.8 105.6 %copy-start.34 = (f32[1088]{0:T(1024)S(1)}, f32[1088]{0:T(1024)}, u32[]{:S(2)}) copy-start(f32[1088]{0:T(1024)} %copy-done.33) | copy-start | bytes 13060
  1006.4 227.4 %copy-start.25 = (f32[4,272]{1,0:T(4,128)S(1)}, f32[4,272]{1,0:T(4,128)}, u32[]{:S(2)}) copy-start(f32[4,272]{1,0:T(4,128)} %get-tuple-element.307) | copy-start | bytes 13060
  1006.4 436.9 %all-gather.20.cloned.1.call-start = ((), (), s32[]{:S(2)}) async-start(), calls=%async_computation.11 | async-start | bytes 2820096 | tf_op jit(solution)/shard_map/all_gather | solution.py:231
  1095.2 360.9 %all-gather.22.cloned.1.call-start = ((), (), s32[]{:S(2)}) async-start(), calls=%async_computation.12 | async-start | bytes 2820096 | tf_op jit(solution)/shard_map/all_gather | solution.py:231
  1233.4 231.2 %all-gather.18.cloned.1.call-start = ((), (), s32[]{:S(2)}) async-start(), calls=%async_computation.10 | async-start | bytes 2820096 | tf_op jit(solution)/shard_map/all_gather | solution.py:231
  (34 other events, 326.5 us)
Sparse Core Ops, SparseCore 0:
  22.1 86.9 all-gather.11
  112.6 82.5 all-gather.13
  197.4 83.5 all-gather.23
  283.0 83.4 all-gather.25
  369.3 82.4 all-gather.15
  792.1 79.4 reduce-scatter.11
  873.9 81.5 reduce-scatter.13
  961.5 133.5 reduce-scatter.17
  1101.3 132.0 reduce-scatter.19
  1239.3 132.0 reduce-scatter.15
  1373.3 28.4 all-gather.19
  1403.5 29.6 all-gather.21
  1435.1 29.4 all-gather.17

commit v2 on v1

v2 whole, which is shorter than its diff:
```python
import numpy as np
import jax
import jax.numpy as jnp
from jax import lax
from jax.experimental import pallas as pl
from jax.experimental.pallas import tpu as pltpu
from jax.sharding import PartitionSpec as P

HD = 64
LANES = 128
EPSILON = 1e-05
F32 = jnp.float32
BF16 = jnp.bfloat16
NT = (((1,), (1,)), ((), ()))
NN = (((1,), (0,)), ((), ()))
TN = (((0,), (0,)), ((), ()))


def dot(left, right, dims):
    return lax.dot_general(left, right, dims, preferred_element_type=F32)


MOVE_A = {
    (0, 0): (0, 0), (0, 1): (0, 1), (0, 3): (1, 0), (0, 2): (1, 1),
    (1, 0): (1, 3), (1, 3): (0, 3), (1, 1): (1, 2), (1, 2): (0, 2),
}
MOVE_B = {
    (0, 0): (1, 0), (0, 1): (1, 1), (0, 3): (0, 0), (0, 2): (0, 1),
    (1, 0): (0, 3), (1, 3): (1, 3), (1, 1): (0, 2), (1, 2): (1, 2),
}


def block_positions():
    spots = {}
    for (_, z), target in MOVE_A.items():
        spots[target] = [2 * z, None]
    for (_, z), target in MOVE_B.items():
        spots[target][1] = 2 * z + 1
    return spots


def task_table():
    spots = block_positions()
    table = np.zeros((2, 4, 18), np.int32)
    for c in range(2):
        for z in range(4):
            members = [(c, z), (1 - c, z), (c, z ^ 1), (1 - c, z ^ 1)]
            slot_of = {}
            for j, member in enumerate(members):
                for half in range(2):
                    slot_of[spots[member][half]] = 2 * j + half
            mine = spots[(c, z)]
            low, high = (0, 1) if mine[0] < mine[1] else (1, 0)
            tasks = [(low, slot_of[mine[low]]), (high, slot_of[mine[high]])]
            tasks += [(high, slot_of[k]) for k in range(4)]
            tasks += [(low, slot_of[k]) for k in range(mine[low])]
            tasks += [(high, slot_of[k]) for k in range(4, mine[high])]
            table[c, z] = [v for pair in tasks for v in pair]
    return table


TASKS = 9


def both_heads(block):
    lane = lax.broadcasted_iota(jnp.int32, block.shape, 1)
    zero = jnp.zeros_like(block)
    return jnp.concatenate(
        [jnp.where(lane < HD, block, zero), jnp.where(lane < HD, zero, block)], 0
    )


def pick_heads(wide, half):
    row = lax.broadcasted_iota(jnp.int32, (LANES, half), 0)
    return jnp.where(row < HD, wide[:, :half], wide[:, half:])


def spread_keys(parts, scratch, half):
    for j, part in enumerate(parts):
        scratch[2 * j] = part[0, :half, :]
        scratch[2 * j + 1] = part[0, half:, :]


def attend_forward(tab, q, k0, k1, k2, k3, v0, v1, v2, v3, out, lse, keys, values_t, queries, scores):
    half = q.shape[1] // 2
    wide = 2 * half
    spread_keys((k0, k1, k2, k3), keys, half)
    for j, part in enumerate((v0, v1, v2, v3)):
        values_t[2 * j] = part[0, :half, :].T
        values_t[2 * j + 1] = part[0, half:, :].T
    scale = jnp.asarray(HD ** (-0.5), BF16)
    for h in range(2):
        queries[h] = both_heads(q[0, h * half : (h + 1) * half, :] * scale)
    key_at = lax.broadcasted_iota(jnp.int32, (half, wide), 0)
    query_at = lax.broadcasted_iota(jnp.int32, (half, wide), 1)
    query_at = jnp.where(query_at < half, query_at, query_at - half)
    low = tab[0]
    high = tab[2]
    peaks = []
    for t in range(TASKS):
        part = dot(keys[tab[2 * t + 1]], queries[tab[2 * t]], NT)
        if t < 2:
            part = jnp.where(key_at <= query_at, part, -1e30)
        scores[t] = part
        peaks.append(jnp.max(part, 0, keepdims=True))
    peak_low = peaks[0]
    peak_high = peaks[1]
    for t in range(2, 6):
        peak_high = jnp.maximum(peak_high, peaks[t])
    is_low = [None] * TASKS
    for t in range(6, TASKS):
        is_low[t] = tab[2 * t] == low
        peak_low = jnp.where(is_low[t], jnp.maximum(peak_low, peaks[t]), peak_low)
        peak_high = jnp.where(is_low[t], peak_high, jnp.maximum(peak_high, peaks[t]))
    total = {0: 0.0, 1: 0.0}
    accum = {0: 0.0, 1: 0.0}
    for t in range(TASKS):
        if t == 0:
            peak = peak_low
        elif t < 6:
            peak = peak_high
        else:
            peak = jnp.where(is_low[t], peak_low, peak_high)
        weights = jnp.exp(scores[t] - peak)
        part_sum = jnp.sum(weights, 0, keepdims=True)
        part_out = dot(values_t[tab[2 * t + 1]], weights.astype(BF16), NN)
        if t == 0:
            total[0] += part_sum
            accum[0] += part_out
        elif t < 6:
            total[1] += part_sum
            accum[1] += part_out
        else:
            total[0] += jnp.where(is_low[t], part_sum, 0.0)
            total[1] += jnp.where(is_low[t], 0.0, part_sum)
            accum[0] += jnp.where(is_low[t], part_out, 0.0)
            accum[1] += jnp.where(is_low[t], 0.0, part_out)
    for which, (spot, peak) in enumerate(((low, peak_low), (high, peak_high))):
        picked = pick_heads(accum[which] / total[which], half)
        out[pl.ds(pl.multiple_of(spot * half, half), half), :] = picked.T.astype(BF16)
        lse[0, spot] = peak + jnp.log(total[which])


def attend_backward(
    tab, q, k0, k1, k2, k3, v0, v1, v2, v3, att, grad, lse,
    dq, dk0, dk1, dk2, dk3, dv0, dv1, dv2, dv3,
    keys, keys_t, values, queries, grads, deltas, key_sums, value_sums, query_sums,
):
    half = q.shape[1] // 2
    wide = 2 * half
    spread_keys((k0, k1, k2, k3), keys, half)
    spread_keys((v0, v1, v2, v3), values, half)
    for slot in range(8):
        keys_t[slot] = keys[slot].T
    scale = jnp.asarray(HD ** (-0.5), BF16)
    for h in range(2):
        rows = slice(h * half, (h + 1) * half)
        queries[h] = both_heads(q[0, rows, :] * scale)
        grads[h] = both_heads(grad[rows, :])
        product = (att[rows, :].astype(F32) * grad[rows, :].astype(F32)).T
        deltas[h] = jnp.concatenate(
            [jnp.sum(product[:HD], 0, keepdims=True), jnp.sum(product[HD:], 0, keepdims=True)], 1
        )
    key_sums[...] = jnp.zeros_like(key_sums)
    value_sums[...] = jnp.zeros_like(value_sums)
    query_sums[...] = jnp.zeros_like(query_sums)
    key_at = lax.broadcasted_iota(jnp.int32, (half, wide), 0)
    query_at = lax.broadcasted_iota(jnp.int32, (half, wide), 1)
    query_at = jnp.where(query_at < half, query_at, query_at - half)
    for t in range(TASKS):
        at = tab[2 * t]
        slot = tab[2 * t + 1]
        query = queries[at]
        upstream = grads[at]
        part = dot(keys[slot], query, NT)
        if t < 2:
            part = jnp.where(key_at <= query_at, part, -1e30)
        probs = jnp.exp(part - lse[0, at])
        grad_probs = dot(values[slot], upstream, NT)
        grad_scores = (probs * (grad_probs - deltas[at])).astype(BF16)
        value_sums[slot] += dot(probs.astype(BF16), upstream, NN)
        key_sums[slot] += dot(grad_scores, query, NN)
        query_sums[at] += dot(keys_t[slot], grad_scores, NN)
    for h in range(2):
        picked = pick_heads(query_sums[h], half) * (HD ** (-0.5))
        dq[h * half : (h + 1) * half, :] = picked.T.astype(BF16)
    for j, (dk, dv) in enumerate(((dk0, dv0), (dk1, dv1), (dk2, dv2), (dk3, dv3))):
        for h in range(2):
            rows = slice(h * half, (h + 1) * half)
            dk[rows, :] = key_sums[2 * j + h].astype(dk.dtype)
            dv[rows, :] = value_sums[2 * j + h].astype(dv.dtype)


def call(kernel, name, grid, in_specs, out_specs, out_shape, scratch=(), prefetch=0):
    return pl.pallas_call(
        kernel,
        name=name,
        grid_spec=pltpu.PrefetchScalarGridSpec(
            num_scalar_prefetch=prefetch,
            grid=grid,
            in_specs=in_specs,
            out_specs=out_specs,
            scratch_shapes=list(scratch),
        ),
        out_shape=out_shape,
        compiler_params=pltpu.CompilerParams(
            dimension_semantics=("arbitrary",) * len(grid), vmem_limit_bytes=60 * 1024 * 1024
        ),
    )


def whole(shape):
    return pl.BlockSpec(shape, lambda *_: (0,) * len(shape))


def sds(shape, dtype):
    return jax.ShapeDtypeStruct(shape, dtype)


def attention_forward(table, mixed, others):
    _, length, width = mixed.shape
    pairs = width // LANES
    half = length // 2

    def column(which):
        return pl.BlockSpec((1, length, LANES), lambda p, tab: (which, 0, p))

    return call(
        attend_forward,
        "attend_forward",
        (pairs,),
        [column(0), column(1)] + [column(0)] * 3 + [column(2)] + [column(1)] * 3,
        [
            pl.BlockSpec((length, LANES), lambda p, tab: (0, p)),
            pl.BlockSpec((1, 2, 1, length), lambda p, tab: (p, 0, 0, 0)),
        ],
        [sds((length, width), BF16), sds((pairs, 2, 1, length), F32)],
        [
            pltpu.VMEM((8, half, LANES), BF16),
            pltpu.VMEM((8, LANES, half), BF16),
            pltpu.VMEM((2, length, LANES), BF16),
            pltpu.VMEM((TASKS, half, length), F32),
        ],
        prefetch=1,
    )(table, mixed, mixed, *others, mixed, *others)


def attention_backward(table, mixed, others, attended, grad_att, lse):
    _, length, width = mixed.shape
    pairs = width // LANES
    half = length // 2

    def column(which):
        return pl.BlockSpec((1, length, LANES), lambda p, tab: (which, 0, p))

    flat = pl.BlockSpec((length, LANES), lambda p, tab: (0, p))
    own = [sds((length, width), F32)]
    sent = [sds((length, width), BF16)] * 3
    return call(
        attend_backward,
        "attend_backward",
        (pairs,),
        [column(0), column(1)]
        + [column(0)] * 3
        + [column(2)]
        + [column(1)] * 3
        + [flat, flat, pl.BlockSpec((1, 2, 1, length), lambda p, tab: (p, 0, 0, 0))],
        [flat] * 9,
        [sds((length, width), BF16)] + own + sent + own + sent,
        [
            pltpu.VMEM((8, half, LANES), BF16),
            pltpu.VMEM((8, LANES, half), BF16),
            pltpu.VMEM((8, half, LANES), BF16),
            pltpu.VMEM((2, length, LANES), BF16),
            pltpu.VMEM((2, length, LANES), BF16),
            pltpu.VMEM((2, 1, length), F32),
            pltpu.VMEM((8, half, LANES), F32),
            pltpu.VMEM((8, half, LANES), F32),
            pltpu.VMEM((2, LANES, length), F32),
        ],
        prefetch=1,
    )(table, mixed, mixed, *others, mixed, *others, attended, grad_att, lse)


def normal_parts(rows):
    centre = rows - jnp.mean(rows, -1, keepdims=True)
    inverse = lax.rsqrt(jnp.mean(centre * centre, -1, keepdims=True) + EPSILON)
    return centre * inverse, inverse


def normal_pull(normal, inverse, grad):
    mean_grad = jnp.mean(grad, -1, keepdims=True)
    mean_both = jnp.mean(grad * normal, -1, keepdims=True)
    return inverse * (grad - mean_grad - normal * mean_both)


def square(block):
    return block[...].reshape(-1, block.shape[-1])


def enter_kernel(x, gain, shift, weight, bias, first, mixed):
    width = mixed.shape[-1]
    features = x.shape[-1]

    @pl.when(pl.program_id(0) == 0)
    def _():
        normal, _ = normal_parts(x[...].astype(F32))
        first[...] = (normal * gain[...] + shift[...]).astype(BF16)

    made = dot(first[...], square(weight), NN) + bias[0]
    mixed[0, :, :features] = made.astype(BF16)
    mixed[0, :, features:] = jnp.zeros((x.shape[0], width - features), BF16)


def enter(x, gain, shift, units, bias):
    length, features = x.shape
    width = -(-features // LANES) * LANES
    unit = (units.shape[0], 1) + units.shape[2:]
    return call(
        enter_kernel,
        "enter",
        (3,),
        [
            whole(x.shape),
            whole((1, features)),
            whole((1, features)),
            pl.BlockSpec(unit, lambda u: (0, u, 0, 0)),
            pl.BlockSpec((1, 1, features), lambda u: (u, 0, 0)),
        ],
        [whole(x.shape), pl.BlockSpec((1, length, width), lambda u: (u, 0, 0))],
        [sds(x.shape, BF16), sds((3, length, width), BF16)],
    )(x, gain, shift, units, bias)


def project_kernel(x, attended, weight, bias, gain, shift, hidden, second):
    features = x.shape[-1]
    branch = dot(attended[:, :features], square(weight), NN) + bias[...]
    stream = x[...].astype(F32) + branch
    hidden[...] = stream
    normal, _ = normal_parts(stream)
    second[...] = (normal * gain[...] + shift[...]).astype(BF16)


def project(x, attended, units, bias, gain, shift):
    length, features = x.shape
    unit = (units.shape[0], 1) + units.shape[2:]
    row = whole((1, features))
    return call(
        project_kernel,
        "project",
        (1,),
        [whole(x.shape), whole(attended.shape), pl.BlockSpec(unit, lambda u: (0, 3, 0, 0)), row, row, row],
        [whole(x.shape), whole(x.shape)],
        [sds(x.shape, F32), sds(x.shape, BF16)],
    )(x, attended, units, bias, gain, shift)


def feed_kernel(
    hidden, second, cot, up, down, up_bias, down_bias,
    result, up_grad, down_grad, up_bias_grad, second_grad, total,
):
    step = pl.program_id(0)
    wide_up = square(up)
    upward = dot(second[...], wide_up, NN) + up_bias[0]
    bell = 0.5 * (1.0 + lax.erf(upward * (0.5**0.5)))
    active = (upward * bell).astype(BF16)
    slope = bell + upward * jnp.exp(-0.5 * upward * upward) * ((0.5 / np.pi) ** 0.5)
    grad_up = (slope * dot(cot[...], down[...], NT)).astype(BF16)
    out_part = dot(active, down[...], NN)
    back_part = dot(grad_up, wide_up, NT)
    down_grad[...] = dot(active, cot[...], TN).astype(BF16)
    up_grad[...] = dot(second[...], grad_up, TN).astype(BF16).reshape(up_grad.shape)
    up_bias_grad[0] = jnp.sum(grad_up.astype(F32), 0, keepdims=True)

    @pl.when(step == 0)
    def _():
        total[...] = hidden[...] + down_bias[...] + out_part
        second_grad[...] = back_part

    @pl.when(step > 0)
    def _():
        total[...] += out_part
        second_grad[...] += back_part

    @pl.when(step == pl.num_programs(0) - 1)
    def _():
        result[...] = total[...].astype(result.dtype)


def feed(hidden, second, cot, up_units, down_full, up_bias, down_bias):
    length, features = hidden.shape
    blocks = up_units.shape[1]
    unit = (up_units.shape[0], 1) + up_units.shape[2:]
    up_spec = pl.BlockSpec(unit, lambda b: (0, b, 0, 0))
    down_spec = pl.BlockSpec((features, features), lambda b: (b, 0))
    row_spec = pl.BlockSpec((1, 1, features), lambda b: (b, 0, 0))
    flat = whole(hidden.shape)
    return call(
        feed_kernel,
        "feed",
        (blocks,),
        [flat, flat, flat, up_spec, down_spec, row_spec, whole((1, features))],
        [flat, up_spec, down_spec, row_spec, flat],
        [
            sds(hidden.shape, BF16),
            sds(up_units.shape, BF16),
            sds(down_full.shape, BF16),
            sds((blocks, 1, features), F32),
            sds(hidden.shape, F32),
        ],
        [pltpu.VMEM(hidden.shape, F32)],
    )(hidden, second, cot, up_units, down_full, up_bias, down_bias)


def turn_kernel(second_grad, hidden, cot, attended, weight, gain, stream_grad, att_grad, out_grad, sums):
    features = hidden.shape[-1]
    width = attended.shape[-1]
    normal, inverse = normal_parts(hidden[...])
    upstream = cot[...].astype(F32)
    grad = second_grad[...]
    stream = upstream + normal_pull(normal, inverse, grad * gain[...])
    stream_grad[...] = stream
    low = stream.astype(BF16)
    made = dot(low, square(weight), NT)
    att_grad[:, :features] = made.astype(BF16)
    att_grad[:, features:] = jnp.zeros((hidden.shape[0], width - features), BF16)
    out_grad[...] = dot(attended[:, :features], low, TN).astype(BF16).reshape(out_grad.shape)
    sums[...] = jnp.concatenate(
        [
            jnp.sum(grad * normal, 0, keepdims=True),
            jnp.sum(grad, 0, keepdims=True),
            jnp.sum(low.astype(F32), 0, keepdims=True),
            jnp.sum(upstream, 0, keepdims=True),
            jnp.zeros((4, features), F32),
        ],
        0,
    )


def turn(second_grad, hidden, cot, attended, units, gain):
    length, features = hidden.shape
    unit = (units.shape[0], 1) + units.shape[2:]
    flat = whole(hidden.shape)
    return call(
        turn_kernel,
        "turn",
        (1,),
        [flat, flat, flat, whole(attended.shape), pl.BlockSpec(unit, lambda u: (0, 3, 0, 0)), whole((1, features))],
        [flat, whole(attended.shape), whole(unit), whole((8, features))],
        [sds(hidden.shape, F32), sds(attended.shape, BF16), sds(unit, BF16), sds((8, features), F32)],
    )(second_grad, hidden, cot, attended, units, gain)


def leave_kernel(mixed_grad, first, x, stream_grad, weight, gain, out_grad, token_grad, unit_grad, column_sums, sums, total):
    step = pl.program_id(0)
    features = x.shape[-1]

    @pl.when(step == 3)
    def _():
        unit_grad[...] = out_grad[...]
        normal, inverse = normal_parts(x[...].astype(F32))
        grad = total[...]
        token_grad[...] = (stream_grad[...] + normal_pull(normal, inverse, grad * gain[...])).astype(BF16)
        sums[...] = jnp.concatenate(
            [jnp.sum(grad * normal, 0, keepdims=True), jnp.sum(grad, 0, keepdims=True), jnp.zeros((6, features), F32)], 0
        )
        column_sums[...] = jnp.zeros_like(column_sums)

    @pl.when(step < 3)
    def _():
        grad = mixed_grad[0, :, :features]
        part = dot(grad, square(weight), NT)
        unit_grad[...] = dot(first[...], grad, TN).astype(BF16).reshape(unit_grad.shape)
        column_sums[0] = jnp.sum(grad.astype(F32), 0, keepdims=True)

        @pl.when(step == 0)
        def _():
            total[...] = part

        @pl.when(step > 0)
        def _():
            total[...] += part


def leave(mixed_grad, first, x, stream_grad, units, gain, out_grad):
    length, features = x.shape
    unit = (units.shape[0], 1) + units.shape[2:]
    flat = whole(x.shape)
    return call(
        leave_kernel,
        "leave",
        (4,),
        [
            pl.BlockSpec((1,) + mixed_grad.shape[1:], lambda u: (jnp.minimum(u, 2), 0, 0)),
            flat,
            flat,
            flat,
            pl.BlockSpec(unit, lambda u: (0, jnp.minimum(u, 2), 0, 0)),
            whole((1, features)),
            whole(unit),
        ],
        [
            flat,
            pl.BlockSpec(unit, lambda u: (0, u, 0, 0)),
            pl.BlockSpec((1, 1, features), lambda u: (u, 0, 0)),
            whole((8, features)),
        ],
        [
            sds(x.shape, BF16),
            sds(units.shape, BF16),
            sds((4, 1, features), F32),
            sds((8, features), F32),
        ],
        [pltpu.VMEM(x.shape, F32)],
    )(mixed_grad, first, x, stream_grad, units, gain, out_grad)


def local(
    tokens, w_qkv, qv_bias, w_out, out_bias, w_up, up_bias, w_down, down_bias,
    ln1_gain, ln1_bias, ln2_gain, ln2_bias, cotangent,
):
    _, length, features = tokens.shape
    rows = w_qkv.shape[0]
    half = length // 2
    reps = lax.axis_size("rep")
    fsdp = lax.axis_size("fsdp")
    rep_at = lax.axis_index("rep")
    z_at = lax.axis_index("fsdp")
    everyone = ("fsdp", "rep")
    grid = ("rep", "fsdp")

    def links(move):
        out = []
        for rep in range(reps):
            for z in range(fsdp):
                parity, target = move(rep % 2, z)
                out.append((rep * fsdp + z, (rep - rep % 2 + parity) * fsdp + target))
        return out

    def turned(perm):
        return [(b, a) for a, b in perm]

    move_a = links(lambda c, z: MOVE_A[(c, z)])
    move_b = links(lambda c, z: MOVE_B[(c, z)])
    to_core = links(lambda c, z: (1 - c, z))
    to_z = links(lambda c, z: (c, z ^ 1))

    def send(value, perm):
        return lax.ppermute(value, grid, perm)

    def swap(value):
        return jnp.concatenate([send(value[:half], move_a), send(value[half:], move_b)], 0)

    def swap_back(value):
        return jnp.concatenate(
            [send(value[:half], turned(move_a)), send(value[half:], turned(move_b))], 0
        )

    table = lax.dynamic_slice(
        jnp.asarray(task_table().reshape(8, -1)), (rep_at % 2 * 4 + z_at, 0), (1, 18)
    ).reshape(-1)

    def own_piece(matrix):
        part = matrix.shape[0] // reps
        return lax.dynamic_slice_in_dim(matrix, rep_at * part, part, 0)

    def to_units(matrix):
        blocks = matrix.shape[1] // features
        return [matrix[:, b * features : (b + 1) * features] for b in range(blocks)]

    def gather_all(matrix):
        return lax.all_gather(own_piece(matrix), everyone, axis=0, tiled=True)

    x = swap(tokens[0])
    cot = swap(cotangent[0])
    units_one = gather_all(jnp.concatenate(to_units(w_qkv) + [w_out], 0)).reshape(fsdp, 4, rows, features)
    units_up = gather_all(jnp.concatenate(to_units(w_up), 0)).reshape(fsdp, -1, rows, features)
    down_full = gather_all(w_down)
    vectors = (qv_bias, out_bias, up_bias, down_bias, ln1_gain, ln1_bias, ln2_gain, ln2_bias)
    small = lax.all_gather(jnp.concatenate(vectors), "fsdp", axis=0).astype(F32)
    pieces = []
    start = 0
    for vector in vectors:
        pieces.append(small[:, start : start + vector.shape[0]].reshape(1, -1))
        start += vector.shape[0]
    qv_full, outb_full, upb_full, downb_full, gain_one, shift_one, gain_two, shift_two = pieces
    bias = jnp.stack([qv_full[:, :features], jnp.zeros((1, features), F32), qv_full[:, features:]])

    first, mixed = enter(x, gain_one, shift_one, units_one, bias)
    pair = mixed[1:]
    from_core = send(pair, to_core)
    from_z = send(pair, to_z)
    others = (from_core, from_z, send(from_z, to_core))
    attended, lse = attention_forward(table, mixed, others)
    hidden, second = project(x, attended, units_one, outb_full, gain_two, shift_two)
    result, up_grad, down_grad, up_bias_grad, second_grad = feed(
        hidden, second, cot, units_up, down_full, upb_full.reshape(-1, 1, features), downb_full
    )
    layer_out = swap_back(result).astype(F32)
    stream_grad, att_grad, out_grad, sums_two = turn(second_grad, hidden, cot, attended, units_one, gain_two)
    att_grad, up_grad, down_grad = lax.optimization_barrier((att_grad, up_grad, down_grad))

    def reduce_part(matrix):
        return lax.psum_scatter(matrix.reshape(-1, features), everyone, scatter_dimension=0, tiled=True)

    def spread_part(part):
        return lax.all_gather(part, "rep", axis=0, tiled=True)

    down_own = spread_part(reduce_part(down_grad)).astype(F32)
    up_own = spread_part(reduce_part(up_grad))

    dq, *rest = attention_backward(table, mixed, others, attended, att_grad, lse)
    dk, dv = rest[:4], rest[4:]
    core_got = [send(jnp.stack([dk[1], dv[1]]), to_core), send(jnp.stack([dk[3], dv[3]]), to_core)]
    z_sum = (jnp.stack([dk[2], dv[2]]).astype(F32) + core_got[1].astype(F32)).astype(BF16)
    z_got = send(z_sum, to_z)
    own = jnp.stack([dk[0], dv[0]]) + core_got[0].astype(F32) + z_got.astype(F32)
    mixed_grad = jnp.concatenate([dq[None], own.astype(BF16)], 0)
    token_low, one_grad, column_sums, sums_one = leave(
        mixed_grad, first, x, stream_grad, units_one, gain_one, out_grad
    )
    grad_tokens = swap_back(token_low).astype(F32)
    one_own = spread_part(reduce_part(one_grad))

    def side_by_side(stack):
        return jnp.concatenate(list(stack), 1).astype(F32)

    up_own = side_by_side(up_own.reshape(-1, rows, features))
    one_own = one_own.reshape(4, rows, features)
    qkv_own = side_by_side(one_own[:3])
    out_own = one_own[3].astype(F32)
    small_grads = (
        jnp.concatenate([column_sums[0], column_sums[2]], 1),
        sums_two[2], up_bias_grad, sums_two[3],
        sums_one[0], sums_one[1], sums_two[0], sums_two[1],
    )
    stacked = jnp.concatenate([g.reshape(fsdp, -1) for g in small_grads], 1)
    stacked = lax.psum(stacked, grid)
    mine = lax.dynamic_index_in_dim(stacked, z_at, 0, keepdims=False)
    small_own = []
    start = 0
    for g in small_grads:
        width = g.size // fsdp
        small_own.append(mine[start : start + width])
        start += width
    return (
        layer_out[None], grad_tokens[None],
        qkv_own, small_own[0], out_own, small_own[1],
        up_own, small_own[2], down_own, small_own[3],
        small_own[4], small_own[5], small_own[6], small_own[7],
    )


def solution(mesh):
    data = P("rep", "fsdp", None)
    matrix = P("fsdp", None)
    vector = P("fsdp")
    return jax.shard_map(
        local,
        mesh=mesh,
        in_specs=(
            data, matrix, vector, matrix, vector, matrix, vector, matrix, vector,
            vector, vector, vector, vector, data,
        ),
        out_specs=(
            data, data, matrix, vector, matrix, vector, matrix, vector, matrix, vector,
            vector, vector, vector, vector,
        ),
        check_vma=False,
    )
```

time: 1500 us -> 946 us (0.63)
  matrix products: 414 us -> 0 us
  local copies, waits for them, and re-layouts: 220 us -> 40.3 us
  Pallas kernels: 0 us -> 162 us
  waiting for transfers between devices: 692 us -> 566 us
  blocking collectives: 61.8 us -> 99.2 us
  starting transfers between devices: 1.31 us -> 32.5 us
  other arithmetic: 57.4 us -> 29.1 us
  loops' own time: 23 us -> 0 us
    dot_general x131 -> x0, matrix products: 414 us -> none  [the longest x34 83.4 us: head_scores(): jnp.einsum('sqd,skd->sqk', query_part, key_part, preferred_element_type=j...]
    ppermute x0 -> x14, waiting for transfers between devices: none -> 206 us  [send(): return lax.ppermute(value, grid, perm)]
    pallas_call x0 -> x7, Pallas kernels: none -> 162 us  [the longest x1 60.6 us: feed(): call(feed_kernel, 'feed', (blocks,), [flat, flat, flat, up_spec, down_spe...]
    all_gather x5 -> x3, waiting for transfers between devices: 143 us -> 0.01 us  [spread_part(): return lax.all_gather(part, 'rep', axis=0, tiled=True)]
    reshape x8, local copies, waits for them, and re-layouts: 105 us -> 5.38 us  [the longest x7 4.18 us: local(): pieces.append(small[:, start:start + vector.shape[0]].reshape(1, -1))]
    reduce_scatter x2 -> x0, waiting for transfers between devices: 97.7 us -> none  [the longest x1 83.9 us: local(): lax.psum_scatter(value_grads.astype(jnp.bfloat16), 'fsdp', scatter_dimens...]
    unnamed x16 -> x12, waiting for transfers between devices: 366 us -> 283 us
    ppermute x0 -> x14, starting transfers between devices: none -> 32.1 us  [send(): return lax.ppermute(value, grid, perm)]
  transfers between devices with their start and end apart: 13 -> 23, of which waited for: 10 -> 11; matrix products, arithmetic and copies ran while one was open for 28% -> 6% of each run, Pallas kernels for 0% -> 10%
where the time goes in v2:
time: 946 us; the launch traced here: 945 us
  waiting for transfers between devices  566 us (60%)
  Pallas kernels  162 us (17%)
  blocking collectives  99.2 us (10%)
  local copies, waits for them, and re-layouts  40.3 us (4%)
  starting transfers between devices  32.5 us (3%)
  other arithmetic  29.1 us (3%)
  between operations  15.2 us (2%)
    unnamed x12, waiting for transfers between devices  283 us
    ppermute x14, waiting for transfers between devices, send(): return lax.ppermute(value, grid, perm)  206 us
    all_gather x3, waiting for transfers between devices, gather_all(): return lax.all_gather(own_piece(matrix), everyone, axis=0, tiled=True)  77.2 us
    psum x1, blocking collectives, local(): stacked = lax.psum(stacked, grid)  61.6 us
    pallas_call x1, Pallas kernels, feed(): call(feed_kernel, 'feed', (blocks,), [flat, flat, flat, up_spec, down_spe...  60.6 us
    unnamed x1, blocking collectives  37.7 us
    pallas_call x1, Pallas kernels, attention_backward(): call(attend_backward, 'attend_backward', (pairs,), [column(0), column(1)]...  34.9 us
    ppermute x14, starting transfers between devices, send(): return lax.ppermute(value, grid, perm)  32.1 us
  transfers between devices with their start and end apart: 23, of which 11 were waited for; matrix products, arithmetic and copies ran while one was open for 6% of the time, Pallas kernels for 10%

profile of v2, /device:TPU:0, one launch (start us, length us, event | category | flops | bytes accessed | tf_op | source)
XLA Modules:
  0.0 944.7 jit_solution(14996262192458613406)
XLA Ops:
  18.1 7.8 collective-permute-start.1
  27.7 37.7 %all-reduce = bf16[13056]{0:T(1024)(128)(2,1)S(1)} all-reduce(bf16[13056]{0:T(1024)(128)(2,1)S(1)} %dynamic-update-slice), channel_id=2, replica_groups=mesh['rep'=8,'fsdp'=4] {'fsdp'}, use_global_device_ids=true, to_apply=%add | all-reduce | flops 13056 | bytes 52224
  69.5 41.3 %all-gather.8.cloned.1.call-done = bf16[4352,1088]{1,0:T(8,128)(2,1)} async-done(((bf16[136,1088]{1,0:T(8,128)(2,1)}), bf16[4352,1088]{1,0:T(8,128)(2,1)}) %all-gather.8.cloned.1.call-update) | async-done | bytes 9469968 | tf_op jit(solution)/shard_map/all_gather | solution.py:572
  110.9 9.8 %enter.1 = (bf16[512,1088]{1,0:T(8,128)(2,1)}, bf16[3,512,1152]{2,1,0:T(8,128)(2,1)}) custom-call(bf16[512,1088]{1,0:T(8,128)(2,1)} %pad_maximum_fusion.3.x, f32[1,1088]{1,0:T(1,128)} %reshape.160.gain, f32[1,1088]{1,0:T(1,128)} %reshape.161.shift, bf16[4,4,272,1088]{3,2,1,0:T(8,128)(2,1)} %bitcast.41, f32[3,1,1088]{2,1,0:T(1,128)} %pad_maximum_fusion.5.bias), custom_call_target="tpu_custom_call" | custom-call | tf_op jit(solution)/shard_map/enter/pallas_call | solution.py:319
  125.4 97.0 %collective-permute-done.3.k2.v2 = bf16[2,512,1152]{2,1,0:T(8,128)(2,1)S(1)} collective-permute-done((bf16[2,512,1152]{2,1,0:T(8,128)(2,1)}, bf16[2,512,1152]{2,1,0:T(8,128)(2,1)S(1)}, u32[]{:S(2)}, u32[]{:S(2)}) %collective-permute-start.3) | collective-permute-done | bytes 2359328 | tf_op jit(solution)/shard_map/ppermute | solution.py:549
  224.9 4.6 collective-permute-start.6
  235.5 11.0 %collective-permute-done.6 = bf16[256,1088]{0,1:T(8,128)(2,1)} collective-permute-done((bf16[256,1088]{0,1:T(8,128)(2,1)}, bf16[256,1088]{0,1:T(8,128)(2,1)}, u32[]{:S(2)}, u32[]{:S(2)}) %collective-permute-start.6) | collective-permute-done | bytes 557088 | tf_op jit(solution)/shard_map/ppermute | solution.py:549
  250.7 21.9 %attend_forward.1 = (bf16[512,1152]{1,0:T(8,128)(2,1)}, f32[9,2,1,512]{3,2,1,0:T(1,128)}) custom-call(s32[18]{0:T(128)} %fusion.9.tab, bf16[3,512,1152]{2,1,0:T(8,128)(2,1)} %get-tuple-element.45.q.k0.v0, bf16[3,512,1152]{2,1,0:T(8,128)(2,1)} %get-tuple-element.45.q.k0.v0, bf16[2,512,1152]{2,1,0:T(8,128)(2,1)} %collective-permute-done.2.k1.v1, ...), custom_call_target="tpu_custom_call" | custom-call | tf_op jit(solution)/shard_map/attend_forward/pallas_call | solution.py:228
  272.6 6.1 project.1
  278.7 35.9 %all-gather.12.cloned.1.call-done.down = bf16[4352,1088]{1,0:T(8,128)(2,1)} async-done(((bf16[136,1088]{1,0:T(8,128)(2,1)}), bf16[4352,1088]{1,0:T(8,128)(2,1)}) %all-gather.12.cloned.1.call-update) | async-done | bytes 9469968 | tf_op jit(solution)/shard_map/all_gather | solution.py:572
  314.6 60.6 %feed.1 = (bf16[512,1088]{1,0:T(8,128)(2,1)}, bf16[4,4,272,1088]{3,2,1,0:T(8,128)(2,1)}, bf16[4352,1088]{1,0:T(8,128)(2,1)}, f32[4,1,1088]{2,1,0:T(1,128)}, f32[512,1088]{1,0:T(8,128)}) custom-call(f32[512,1088]{1,0:T(8,128)} %get-tuple-element.47.hidden, bf16[512,1088]{1,0:T(8,128)(2,1)} %get-tuple-element.48.second, ...), custom_call_target="tpu_custom_call" | custom-call | tf_op jit(solution)/shard_map/feed/pallas_call | solution.py:398
  375.2 10.0 %turn.1 = (f32[512,1088]{1,0:T(8,128)}, bf16[512,1152]{1,0:T(8,128)(2,1)}, bf16[4,1,272,1088]{3,2,1,0:T(8,128)(2,1)}, f32[8,1088]{1,0:T(8,128)}) custom-call(f32[512,1088]{1,0:T(8,128)} %get-tuple-element.50.second_grad, f32[512,1088]{1,0:T(8,128)} %get-tuple-element.47.hidden, bf16[512,1088]{1,0:T(8,128)(2,1)} %pad_maximum_fusion.4.cot, ...), custom_call_target="tpu_custom_call" | custom-call | tf_op jit(solution)/shard_map/turn/pallas_call | solution.py:444
  385.9 34.9 %attend_backward.1 = (bf16[512,1152]{1,0:T(8,128)(2,1)}, f32[512,1152]{1,0:T(8,128)}, bf16[512,1152]{1,0:T(8,128)(2,1)}, bf16[512,1152]{1,0:T(8,128)(2,1)}, bf16...) custom-call(s32[18]{0:T(128)} %fusion.9.tab, ...), custom_call_target="tpu_custom_call" | custom-call | tf_op jit(solution)/shard_map/attend_backward/pallas_call | solution.py:259
  430.8 83.9 %collective-permute-done.11 = bf16[2,512,1152]{2,1,0:T(8,128)(2,1)S(1)} collective-permute-done((bf16[2,512,1152]{2,1,0:T(8,128)(2,1)S(1)}, bf16[2,512,1152]{2,1,0:T(8,128)(2,1)S(1)}, u32[]{:S(2)}, u32[]{:S(2)}) %collective-permute-start.11) | collective-permute-done | bytes 2359328 | tf_op jit(solution)/shard_map/ppermute | solution.py:549
  518.1 18.9 %leave.1 = (bf16[512,1088]{1,0:T(8,128)(2,1)}, bf16[4,4,272,1088]{3,2,1,0:T(8,128)(2,1)}, f32[4,1,1088]{2,1,0:T(1,128)}, f32[8,1088]{1,0:T(8,128)}) custom-call(bf16[3,512,1152]{2,1,0:T(8,128)(2,1)} %pad_maximum_fusion.mixed_grad, bf16[512,1088]{1,0:T(8,128)(2,1)} %get-tuple-element.65.first, bf16[512,1088]{1,0:T(8,128)(2,1)} %pad_maximum_fusion.3.x, ...), custom_call_target="tpu_custom_call" | custom-call | tf_op jit(solution)/shard_map/leave/pallas_call | solution.py:489
  537.1 6.6 reduce-scatter.12.cloned.1.call-done
  543.7 137.8 %reduce-scatter.14.cloned.1.call-done = bf16[136,1088]{1,0:T(8,128)(2,1)} async-done(((bf16[4352,1088]{1,0:T(8,128)(2,1)}), bf16[136,1088]{1,0:T(8,128)(2,1)}) %reduce-scatter.14.cloned.1.call-update) | async-done | bytes 295952
  681.6 137.9 %reduce-scatter.10.cloned.1.call-done = bf16[136,1088]{1,0:T(8,128)(2,1)} async-done(((bf16[4352,1088]{1,0:T(8,128)(2,1)}), bf16[136,1088]{1,0:T(8,128)(2,1)}) %reduce-scatter.10.cloned.1.call-update) | async-done | bytes 295952
  822.0 5.2 collective-permute-start.8
  827.6 9.0 collective-permute-done.8
  839.6 7.4 collective-permute-start.13
  848.3 61.6 %psum.7 = f32[4,3264]{1,0:T(4,128)S(1)} all-reduce(f32[4,3264]{1,0:T(4,128)S(1)} %concatenate.72), channel_id=1, replica_groups=mesh['rep'=8,'fsdp'=4] {'rep','fsdp'}, use_global_device_ids=true, to_apply=%region_1.2 | all-reduce | flops 13056 | bytes 104448 | tf_op jit(solution)/shard_map/psum | solution.py:638
  922.9 4.3 convert_element_type.65
  930.4 4.0 concatenate.70
  (160 shorter events, 74.5 us)
Async XLA Ops:
  7.2 103.7 %all-gather.8.cloned.1.call-start = ((), (), s32[]{:S(2)}) async-start(), calls=%async_computation.3 | async-start | bytes 10340352 | tf_op jit(solution)/shard_map/all_gather | solution.py:572
  11.4 267.4 %all-gather.10.cloned.1.call-start = ((), (), s32[]{:S(2)}) async-start(), calls=%async_computation.4 | async-start | bytes 10340352 | tf_op jit(solution)/shard_map/all_gather | solution.py:572
  15.2 299.4 %all-gather.12.cloned.1.call-start = ((), (), s32[]{:S(2)}) async-start(), calls=%async_computation.5 | async-start | bytes 10340352 | tf_op jit(solution)/shard_map/all_gather | solution.py:572
  16.1 527.5 %reduce-scatter.12.cloned.1.call-start = ((), (), s32[]{:S(2)}) async-start(), calls=%async_computation.10 | async-start | bytes 10340352
  17.4 50.4 %collective-permute-start = (bf16[256,1088]{0,1:T(8,128)(2,1)S(1)}, bf16[256,1088]{0,1:T(8,128)(2,1)S(1)}, u32[]{:S(2)}, u32[]{:S(2)}) collective-permute-start(bf16[256,1088]{0,1:T(8,128)(2,1)S(1)} %get-tuple-element.123), channel_id=1, source_target_pairs={{0,0},{1,1},{2,5},{3,4},{4,7},{5,6},{6,2},{7,3},{8,8},{9,9},{10,13... | collective-permute-start | bytes 1671176 | tf_op jit(solution)/shard_map/ppermute | solution.py:549
  18.1 50.0 %collective-permute-start.1 = (bf16[256,1088]{0,1:T(8,128)(2,1)S(1)}, bf16[256,1088]{0,1:T(8,128)(2,1)S(1)}, u32[]{:S(2)}, u32[]{:S(2)}) collective-permute-start(bf16[256,1088]{0,1:T(8,128)(2,1)S(1)} %get-tuple-element.124), channel_id=1, source_target_pairs={{0,4},{1,5},{2,1},{3,0},{4,3},{5,2},{6,6},{7,7},{8,12},{9,13},{10,... | collective-permute-start | bytes 1671176 | tf_op jit(solution)/shard_map/ppermute | solution.py:549
  124.1 98.4 %collective-permute-start.3 = (bf16[2,512,1152]{2,1,0:T(8,128)(2,1)}, bf16[2,512,1152]{2,1,0:T(8,128)(2,1)S(1)}, u32[]{:S(2)}, u32[]{:S(2)}) collective-permute-start(bf16[2,512,1152]{2,1,0:T(8,128)(2,1)} %slice.190), channel_id=1, source_target_pairs={{0,1},{1,0},{2,3},{3,2},{4,5},{5,4},{6,7},{7,6},{8,9},{9,8},{10,11... | collective-permute-start | bytes 7077896 | tf_op jit(solution)/shard_map/ppermute | solution.py:549
  125.4 125.3 %collective-permute-start.2 = (bf16[2,512,1152]{2,1,0:T(8,128)(2,1)}, bf16[2,512,1152]{2,1,0:T(8,128)(2,1)}, u32[]{:S(2)}, u32[]{:S(2)}) collective-permute-start(bf16[2,512,1152]{2,1,0:T(8,128)(2,1)} %slice.190), channel_id=1, source_target_pairs={{0,4},{1,5},{2,6},{3,7},{4,0},{5,1},{6,2},{7,3},{8,12},{9,13},{10,... | collective-permute-start | bytes 7077896 | tf_op jit(solution)/shard_map/ppermute | solution.py:549
  222.5 28.3 %collective-permute-start.4 = (bf16[2,512,1152]{2,1,0:T(8,128)(2,1)S(1)}, bf16[2,512,1152]{2,1,0:T(8,128)(2,1)}, u32[]{:S(2)}, u32[]{:S(2)}) collective-permute-start(bf16[2,512,1152]{2,1,0:T(8,128)(2,1)S(1)} %collective-permute-done.3.k2.v2), channel_id=1, source_target_pairs={{0,4},{1,5},{2,6},{3,7},{4,0},{5,1},{6,2},{7,3},{8,12},{9,13},{10,... | collective-permute-start | bytes 7077896 | tf_op jit(solution)/shard_map/ppermute | solution.py:549
  223.5 10.6 %collective-permute-start.5 = (bf16[256,1088]{0,1:T(8,128)(2,1)S(1)}, bf16[256,1088]{0,1:T(8,128)(2,1)}, u32[]{:S(2)}, u32[]{:S(2)}) collective-permute-start(bf16[256,1088]{0,1:T(8,128)(2,1)S(1)} %get-tuple-element.121), channel_id=1, source_target_pairs={{0,0},{1,1},{2,5},{3,4},{4,7},{5,6},{6,2},{7,3},{8,8},{9,9},{10,13... | collective-permute-start | bytes 1671176 | tf_op jit(solution)/shard_map/ppermute | solution.py:549
  224.9 21.5 %collective-permute-start.6 = (bf16[256,1088]{0,1:T(8,128)(2,1)}, bf16[256,1088]{0,1:T(8,128)(2,1)}, u32[]{:S(2)}, u32[]{:S(2)}) collective-permute-start(bf16[256,1088]{0,1:T(8,128)(2,1)} %get-tuple-element.122), channel_id=1, source_target_pairs={{0,4},{1,5},{2,1},{3,0},{4,3},{5,2},{6,6},{7,7},{8,12},{9,13},{10,... | collective-permute-start | bytes 1671176 | tf_op jit(solution)/shard_map/ppermute | solution.py:549
  385.2 296.3 %reduce-scatter.14.cloned.1.call-start = ((), (), s32[]{:S(2)}) async-start(), calls=%async_computation.11 | async-start | bytes 10340352
  385.8 433.7 %reduce-scatter.10.cloned.1.call-start = ((), (), s32[]{:S(2)}) async-start(), calls=%async_computation.9 | async-start | bytes 10340352
  422.8 4.6 collective-permute-start.10
  423.3 7.4 collective-permute-start.9
  428.0 86.7 %collective-permute-start.11 = (bf16[2,512,1152]{2,1,0:T(8,128)(2,1)S(1)}, bf16[2,512,1152]{2,1,0:T(8,128)(2,1)S(1)}, u32[]{:S(2)}, u32[]{:S(2)}) collective-permute-start(bf16[2,512,1152]{2,1,0:T(8,128)(2,1)S(1)} %add_convert_fusion), channel_id=1, source_target_pairs={{0,1},{1,0},{2,3},{3,2},{4,5},{5,4},{6,7},{7,6},{8,9},{9,8},{10,11... | collective-permute-start | bytes 7077896 | tf_op jit(solution)/shard_map/ppermute | solution.py:549
  537.0 282.6 %copy-start.8 = (bf16[512,1088]{1,0:T(8,128)(2,1)S(1)}, bf16[512,1088]{1,0:T(8,128)(2,1)}, u32[]{:S(2)}) copy-start(bf16[512,1088]{1,0:T(8,128)(2,1)} %get-tuple-element.49) | copy-start | bytes 3342340
  537.0 376.5 %all-gather.16.cloned.1.call-start = ((), (), s32[]{:S(2)}) async-start(), calls=%async_computation.7 | async-start | bytes 2820096 | tf_op jit(solution)/shard_map/all_gather | solution.py:607
  543.6 379.3 %all-gather.18.cloned.1.call-start = ((), (), s32[]{:S(2)}) async-start(), calls=%async_computation.8 | async-start | bytes 2820096 | tf_op jit(solution)/shard_map/all_gather | solution.py:607
  681.6 245.7 %all-gather.14.cloned.1.call-start = ((), (), s32[]{:S(2)}) async-start(), calls=%async_computation.6 | async-start | bytes 2820096 | tf_op jit(solution)/shard_map/all_gather | solution.py:607
  819.9 7.7 collective-permute-start.7
  822.0 14.6 %collective-permute-start.8 = (bf16[256,1088]{0,1:T(8,128)(2,1)}, bf16[256,1088]{0,1:T(8,128)(2,1)S(1)}, u32[]{:S(2)}, u32[]{:S(2)}) collective-permute-start(bf16[256,1088]{0,1:T(8,128)(2,1)} %copy.40), channel_id=1, source_target_pairs={{4,0},{5,1},{1,2},{0,3},{3,4},{2,5},{6,6},{7,7},{12,8},{13,9},{9,1... | collective-permute-start | bytes 1671176 | tf_op jit(solution)/shard_map/ppermute | solution.py:549
  838.6 73.2 %collective-permute-start.12 = (bf16[256,1088]{0,1:T(8,128)(2,1)S(1)}, bf16[256,1088]{0,1:T(8,128)(2,1)S(1)}, u32[]{:S(2)}, u32[]{:S(2)}) collective-permute-start(bf16[256,1088]{0,1:T(8,128)(2,1)S(1)} %copy.41), channel_id=1, source_target_pairs={{0,0},{1,1},{5,2},{4,3},{7,4},{6,5},{2,6},{3,7},{8,8},{9,9},{13,10... | collective-permute-start | bytes 1671176 | tf_op jit(solution)/shard_map/ppermute | solution.py:549
  839.6 72.3 %collective-permute-start.13 = (bf16[256,1088]{0,1:T(8,128)(2,1)S(1)}, bf16[256,1088]{0,1:T(8,128)(2,1)S(1)}, u32[]{:S(2)}, u32[]{:S(2)}) collective-permute-start(bf16[256,1088]{0,1:T(8,128)(2,1)S(1)} %copy.42), channel_id=1, source_target_pairs={{4,0},{5,1},{1,2},{0,3},{3,4},{2,5},{6,6},{7,7},{12,8},{13,9},{9,1... | collective-permute-start | bytes 1671176 | tf_op jit(solution)/shard_map/ppermute | solution.py:549
  (24 other events, 484.4 us)
Sparse Core Ops, SparseCore 0:
  11.5 99.3 all-gather.7
  113.8 107.4 all-gather.9
  224.2 90.3 all-gather.11
  385.4 158.2 reduce-scatter.11
  549.6 131.9 reduce-scatter.13
  687.5 131.9 reduce-scatter.9
  821.4 28.2 all-gather.15
  851.6 30.0 all-gather.17
  883.5 30.0 all-gather.13

commit v3 on v2

v3 whole, which is shorter than its diff:
```python
import functools

import numpy as np
import jax
import jax.numpy as jnp
from jax import lax
from jax.experimental import pallas as pl
from jax.experimental.pallas import tpu as pltpu
from jax.sharding import PartitionSpec as P


HD = 64
LANES = 128
EPSILON = 1e-05
F32 = jnp.float32
BF16 = jnp.bfloat16
NT = (((1,), (1,)), ((), ()))
NN = (((1,), (0,)), ((), ()))
TN = (((0,), (0,)), ((), ()))


def dot(left, right, dims):
    return lax.dot_general(left, right, dims, preferred_element_type=F32)


def owner(block):
    return min(block, 7 - block)


def destination(pick, z, half):
    index = owner(2 * z + half)
    return index % 2, index // 2 if pick == 0 else 3 - index // 2


def task_table():
    def held(index):
        return [b for h in range(2) for b in range(h, 8, 2) if owner(b) == index]

    table = np.zeros((4, 18), np.int32)
    for me in range(4):
        slot_of = {}
        for j, member in enumerate((me, me ^ 1, me ^ 2, me ^ 3)):
            for half in range(2):
                slot_of[held(member)[half]] = 2 * j + half
        mine = held(me)
        low, high = (0, 1) if mine[0] < mine[1] else (1, 0)
        tasks = [(low, slot_of[mine[low]]), (high, slot_of[mine[high]])]
        tasks += [(high, slot_of[k]) for k in range(4)]
        tasks += [(low, slot_of[k]) for k in range(mine[low])]
        tasks += [(high, slot_of[k]) for k in range(4, mine[high])]
        table[me] = [v for pair in tasks for v in pair]
    return table


TASKS = 9


def both_heads(block):
    lane = lax.broadcasted_iota(jnp.int32, block.shape, 1)
    zero = jnp.zeros_like(block)
    return jnp.concatenate(
        [jnp.where(lane < HD, block, zero), jnp.where(lane < HD, zero, block)], 0
    )


def pick_heads(wide, half):
    row = lax.broadcasted_iota(jnp.int32, (LANES, half), 0)
    return jnp.where(row < HD, wide[:, :half], wide[:, half:])


def spread_keys(parts, scratch, half):
    for j, part in enumerate(parts):
        scratch[2 * j] = part[0, :half, :]
        scratch[2 * j + 1] = part[0, half:, :]


def attend_forward(tab, q, k0, k1, k2, k3, v0, v1, v2, v3, out, lse, keys, values_t, queries, scores):
    half = q.shape[0] // 2
    wide = 2 * half
    spread_keys((k0, k1, k2, k3), keys, half)
    for j, part in enumerate((v0, v1, v2, v3)):
        values_t[2 * j] = part[0, :half, :].T
        values_t[2 * j + 1] = part[0, half:, :].T
    scale = jnp.asarray(HD ** (-0.5), BF16)
    for h in range(2):
        queries[h] = both_heads(q[h * half : (h + 1) * half, :] * scale)
    key_at = lax.broadcasted_iota(jnp.int32, (half, wide), 0)
    query_at = lax.broadcasted_iota(jnp.int32, (half, wide), 1)
    query_at = jnp.where(query_at < half, query_at, query_at - half)
    low = tab[0]
    high = tab[2]
    peaks = []
    for t in range(TASKS):
        part = dot(keys[tab[2 * t + 1]], queries[tab[2 * t]], NT)
        if t < 2:
            part = jnp.where(key_at <= query_at, part, -1e30)
        scores[t] = part
        peaks.append(jnp.max(part, 0, keepdims=True))
    peak_low = peaks[0]
    peak_high = peaks[1]
    for t in range(2, 6):
        peak_high = jnp.maximum(peak_high, peaks[t])
    is_low = [None] * TASKS
    for t in range(6, TASKS):
        is_low[t] = tab[2 * t] == low
        peak_low = jnp.where(is_low[t], jnp.maximum(peak_low, peaks[t]), peak_low)
        peak_high = jnp.where(is_low[t], peak_high, jnp.maximum(peak_high, peaks[t]))
    total = {0: 0.0, 1: 0.0}
    accum = {0: 0.0, 1: 0.0}
    for t in range(TASKS):
        if t == 0:
            peak = peak_low
        elif t < 6:
            peak = peak_high
        else:
            peak = jnp.where(is_low[t], peak_low, peak_high)
        weights = jnp.exp(scores[t] - peak)
        part_sum = jnp.sum(weights, 0, keepdims=True)
        part_out = dot(values_t[tab[2 * t + 1]], weights.astype(BF16), NN)
        if t == 0:
            total[0] += part_sum
            accum[0] += part_out
        elif t < 6:
            total[1] += part_sum
            accum[1] += part_out
        else:
            total[0] += jnp.where(is_low[t], part_sum, 0.0)
            total[1] += jnp.where(is_low[t], 0.0, part_sum)
            accum[0] += jnp.where(is_low[t], part_out, 0.0)
            accum[1] += jnp.where(is_low[t], 0.0, part_out)
    for which, (spot, peak) in enumerate(((low, peak_low), (high, peak_high))):
        picked = pick_heads(accum[which] / total[which], half)
        out[pl.ds(pl.multiple_of(spot * half, half), half), :] = picked.T.astype(BF16)
        lse[0, spot] = peak + jnp.log(total[which])


def attend_backward(
    tab, q, k0, k1, k2, k3, v0, v1, v2, v3, att, grad, lse,
    dq, pair0, pair1, pair2, pair3,
    keys, keys_t, values, queries, grads, deltas, key_sums, value_sums, query_sums,
):
    half = q.shape[0] // 2
    wide = 2 * half
    spread_keys((k0, k1, k2, k3), keys, half)
    spread_keys((v0, v1, v2, v3), values, half)
    for slot in range(8):
        keys_t[slot] = keys[slot].T
    scale = jnp.asarray(HD ** (-0.5), BF16)
    for h in range(2):
        rows = slice(h * half, (h + 1) * half)
        queries[h] = both_heads(q[rows, :] * scale)
        grads[h] = both_heads(grad[rows, :])
        product = (att[rows, :].astype(F32) * grad[rows, :].astype(F32)).T
        deltas[h] = jnp.concatenate(
            [jnp.sum(product[:HD], 0, keepdims=True), jnp.sum(product[HD:], 0, keepdims=True)], 1
        )
    key_sums[...] = jnp.zeros_like(key_sums)
    value_sums[...] = jnp.zeros_like(value_sums)
    query_sums[...] = jnp.zeros_like(query_sums)
    key_at = lax.broadcasted_iota(jnp.int32, (half, wide), 0)
    query_at = lax.broadcasted_iota(jnp.int32, (half, wide), 1)
    query_at = jnp.where(query_at < half, query_at, query_at - half)
    for t in range(TASKS):
        at = tab[2 * t]
        slot = tab[2 * t + 1]
        query = queries[at]
        upstream = grads[at]
        part = dot(keys[slot], query, NT)
        if t < 2:
            part = jnp.where(key_at <= query_at, part, -1e30)
        probs = jnp.exp(part - lse[0, at])
        grad_probs = dot(values[slot], upstream, NT)
        grad_scores = (probs * (grad_probs - deltas[at])).astype(BF16)
        value_sums[slot] += dot(probs.astype(BF16), upstream, NN)
        key_sums[slot] += dot(grad_scores, query, NN)
        query_sums[at] += dot(keys_t[slot], grad_scores, NN)
    for h in range(2):
        picked = pick_heads(query_sums[h], half) * (HD ** (-0.5))
        dq[h * half : (h + 1) * half, :] = picked.T.astype(BF16)
    for j, pair in enumerate((pair0, pair1, pair2, pair3)):
        for h in range(2):
            rows = slice(h * half, (h + 1) * half)
            pair[0, rows, :] = key_sums[2 * j + h].astype(pair.dtype)
            pair[1, rows, :] = value_sums[2 * j + h].astype(pair.dtype)


def call(kernel, grid, in_specs, out_specs, out_shape, scratch=(), prefetch=0):
    return pl.pallas_call(
        kernel,
        grid_spec=pltpu.PrefetchScalarGridSpec(
            num_scalar_prefetch=prefetch,
            grid=grid,
            in_specs=in_specs,
            out_specs=out_specs,
            scratch_shapes=list(scratch),
        ),
        out_shape=out_shape,
        compiler_params=pltpu.CompilerParams(
            dimension_semantics=("arbitrary",) * len(grid), vmem_limit_bytes=60 * 1024 * 1024
        ),
    )


def whole(shape):
    return pl.BlockSpec(shape, lambda *_: (0,) * len(shape))


def sds(shape, dtype):
    return jax.ShapeDtypeStruct(shape, dtype)


def attention_inputs(queries, pair, others):
    length, _ = queries.shape

    def column(which):
        return pl.BlockSpec((1, length, LANES), lambda p, tab: (which, 0, p))

    flat = pl.BlockSpec((length, LANES), lambda p, tab: (0, p))
    return [flat] + [column(0)] * 4 + [column(1)] * 4, (queries, pair, *others, pair, *others)


def attention_forward(table, queries, pair, others):
    length, width = queries.shape
    pairs = width // LANES
    half = length // 2
    specs, operands = attention_inputs(queries, pair, others)
    return call(
        attend_forward,
        (pairs,),
        specs,
        [
            pl.BlockSpec((length, LANES), lambda p, tab: (0, p)),
            pl.BlockSpec((1, 2, 1, length), lambda p, tab: (p, 0, 0, 0)),
        ],
        [sds((length, width), BF16), sds((pairs, 2, 1, length), F32)],
        [
            pltpu.VMEM((8, half, LANES), BF16),
            pltpu.VMEM((8, LANES, half), BF16),
            pltpu.VMEM((2, length, LANES), BF16),
            pltpu.VMEM((TASKS, half, length), F32),
        ],
        prefetch=1,
    )(table, *operands)


def attention_backward(table, queries, pair, others, attended, grad_att, lse):
    length, width = queries.shape
    pairs = width // LANES
    half = length // 2
    specs, operands = attention_inputs(queries, pair, others)
    flat = pl.BlockSpec((length, LANES), lambda p, tab: (0, p))
    both = pl.BlockSpec((2, length, LANES), lambda p, tab: (0, 0, p))
    return call(
        attend_backward,
        (pairs,),
        specs + [flat, flat, pl.BlockSpec((1, 2, 1, length), lambda p, tab: (p, 0, 0, 0))],
        [flat] + [both] * 4,
        [sds((length, width), BF16), sds((2, length, width), F32)] + [sds((2, length, width), BF16)] * 3,
        [
            pltpu.VMEM((8, half, LANES), BF16),
            pltpu.VMEM((8, LANES, half), BF16),
            pltpu.VMEM((8, half, LANES), BF16),
            pltpu.VMEM((2, length, LANES), BF16),
            pltpu.VMEM((2, length, LANES), BF16),
            pltpu.VMEM((2, 1, length), F32),
            pltpu.VMEM((8, half, LANES), F32),
            pltpu.VMEM((8, half, LANES), F32),
            pltpu.VMEM((2, LANES, length), F32),
        ],
        prefetch=1,
    )(table, *operands, attended, grad_att, lse)


def normal_parts(rows):
    centre = rows - jnp.mean(rows, -1, keepdims=True)
    inverse = lax.rsqrt(jnp.mean(centre * centre, -1, keepdims=True) + EPSILON)
    return centre * inverse, inverse


def normal_pull(normal, inverse, grad):
    mean_grad = jnp.mean(grad, -1, keepdims=True)
    mean_both = jnp.mean(grad * normal, -1, keepdims=True)
    return inverse * (grad - mean_grad - normal * mean_both)


def square(block):
    return block[...].reshape(-1, block.shape[-1])


CHUNK_STARTS = (0, 72, 136, 200)
CHUNK = 72


def chunk_start(quarter):
    return jnp.where(
        quarter < 2,
        jnp.where(quarter == 0, CHUNK_STARTS[0], CHUNK_STARTS[1]),
        jnp.where(quarter == 2, CHUNK_STARTS[2], CHUNK_STARTS[3]),
    )


def assemble_kernel(spot, near, far, out, *, by_z):
    features = out.shape[-1]
    for other, pieces in enumerate((near, far)):

        @pl.when(pl.program_id(0) % 2 ^ spot[0] == other)
        def _(pieces=pieces):
            for order in range(4):
                start = pl.multiple_of(chunk_start(spot[1] ^ order), 8)
                for back in range(4):
                    z = (spot[2] + 4 - back) % 4
                    made = pieces[order, back, 0, :, :features]
                    if by_z:
                        out[z, 0, pl.ds(start, CHUNK), :] = made
                    else:
                        out[0, z, pl.ds(start, CHUNK), :] = made


def assemble(spot, pieces, rows, features, by_z=False):
    units = 2 * pieces[0].shape[2]
    part = pieces[0].shape[:2] + (1,) + pieces[0].shape[3:]
    if by_z:
        spec = pl.BlockSpec((4, 1, rows, features), lambda u, spot: (0, u, 0, 0))
        shape = (4, units, rows, features)
    else:
        spec = pl.BlockSpec((1, 4, rows, features), lambda u, spot: (u, 0, 0, 0))
        shape = (units, 4, rows, features)
    return call(
        functools.partial(assemble_kernel, by_z=by_z),
        (units,),
        [pl.BlockSpec(part, lambda u, spot: (0, 0, u // 2, 0, 0)) for p in pieces],
        spec,
        sds(shape, BF16),
        prefetch=1,
    )(spot, *pieces)


def finish_kernel(spot, *refs, units, across):
    groups = len(units)
    outs = refs[groups:]
    for pieces, group, outs_of in zip(refs[:groups], units, across):
        for unit, (target, place) in enumerate(zip(group, outs_of)):
            out = outs[target]
            features = pieces.shape[-1] if place is None else place[2]
            for order in range(4):
                start = pl.multiple_of(chunk_start(spot[1] ^ order), 8)
                made = pieces[spot[0] ^ (unit % 2), order, unit // 2, :, :features].astype(F32)
                row, column, _ = place
                out[pl.ds(row + start, CHUNK), column : column + features] = made


def finish(spot, groups, shapes, units, places):
    return call(
        functools.partial(finish_kernel, units=units, across=places),
        (1,),
        [pl.BlockSpec(g.shape, lambda u, spot, n=g.ndim: (0,) * n) for g in groups],
        [pl.BlockSpec(shape, lambda u, spot: (0, 0)) for shape in shapes],
        [sds(shape, F32) for shape in shapes],
        prefetch=1,
    )(spot, *groups)


def enter_kernel(x, gain, shift, weight, bias, first, mixed):
    width = mixed.shape[-1]
    features = first.shape[-1]

    @pl.when(pl.program_id(0) == 0)
    def _():
        normal, _ = normal_parts(x[:, : first.shape[-1]].astype(F32))
        first[...] = (normal * gain[...] + shift[...]).astype(BF16)

    made = dot(first[...], square(weight), NN) + bias[0]
    mixed[0, :, :features] = made.astype(BF16)
    mixed[0, :, features:] = jnp.zeros((x.shape[0], width - features), BF16)


def unit_spec(weights, pick):
    shape = (1,) + weights.shape[1:]
    return pl.BlockSpec(shape, lambda *at: (pick(*at), 0, 0, 0))


def enter(x, gain, shift, weights, bias):
    length, width = x.shape
    features = weights.shape[-1]
    return call(
        enter_kernel,
        (2,),
        [
            whole(x.shape),
            whole((1, features)),
            whole((1, features)),
            unit_spec(weights, lambda u: u),
            pl.BlockSpec((1, 1, features), lambda u: (u, 0, 0)),
        ],
        [whole((length, features)), pl.BlockSpec((1, length, width), lambda u: (u, 0, 0))],
        [sds((length, features), BF16), sds((2, length, width), BF16)],
    )(x, gain, shift, weights, bias)


def query_kernel(first, weight, bias, out):
    features = first.shape[-1]
    made = dot(first[...], square(weight), NN) + bias[...]
    out[:, :features] = made.astype(BF16)
    out[:, features:] = jnp.zeros((out.shape[0], out.shape[1] - features), BF16)


def query(first, weights, bias):
    length, features = first.shape
    width = -(-features // LANES) * LANES
    return call(
        query_kernel,
        (1,),
        [whole(first.shape), unit_spec(weights, lambda u: 0), whole((1, features))],
        whole((length, width)),
        sds((length, width), BF16),
    )(first, weights, bias)


def project_kernel(x, attended, weight, bias, gain, shift, hidden, second):
    features = hidden.shape[-1]
    branch = dot(attended[:, :features], square(weight), NN) + bias[...]
    stream = x[:, :features].astype(F32) + branch
    hidden[...] = stream
    normal, _ = normal_parts(stream)
    second[...] = (normal * gain[...] + shift[...]).astype(BF16)


def project(x, attended, weights, bias, gain, shift):
    length, features = x.shape[0], weights.shape[-1]
    row = whole((1, features))
    return call(
        project_kernel,
        (1,),
        [whole(x.shape), whole(attended.shape), unit_spec(weights, lambda u: 1), row, row, row],
        [whole((length, features)), whole((length, features))],
        [sds((length, features), F32), sds((length, features), BF16)],
    )(x, attended, weights, bias, gain, shift)


def feed_kernel(
    hidden, second, cot, up, down, up_bias, down_bias,
    result, up_grad, down_grad, up_bias_grad, second_grad, total,
):
    step = pl.program_id(0)
    features = hidden.shape[-1]
    cot = cot[:, :features]
    wide_up = square(up)
    wide_down = square(down)
    upward = dot(second[...], wide_up, NN) + up_bias[0]
    bell = 0.5 * (1.0 + lax.erf(upward * (0.5**0.5)))
    active = (upward * bell).astype(BF16)
    slope = bell + upward * jnp.exp(-0.5 * upward * upward) * ((0.5 / np.pi) ** 0.5)
    grad_up = (slope * dot(cot, wide_down, NT)).astype(BF16)
    out_part = dot(active, wide_down, NN)
    back_part = dot(grad_up, wide_up, NT)
    store_units(down_grad, dot(active, cot, TN))
    store_units(up_grad, dot(second[...], grad_up, TN))
    up_bias_grad[0] = jnp.sum(grad_up.astype(F32), 0, keepdims=True)

    @pl.when(step == 0)
    def _():
        total[...] = hidden[...] + down_bias[...] + out_part
        second_grad[...] = back_part

    @pl.when(step > 0)
    def _():
        total[...] += out_part
        second_grad[...] += back_part

    @pl.when(step == pl.num_programs(0) - 1)
    def _():
        result[:, :features] = total[...].astype(result.dtype)
        result[:, features:] = jnp.zeros((result.shape[0], result.shape[1] - features), result.dtype)


def feed(hidden, second, cot, up_weights, down_full, up_bias, down_bias):
    length, features = hidden.shape
    blocks, fsdp, rows, _ = up_weights.shape
    width = -(-features // LANES) * LANES
    row_spec = pl.BlockSpec((1, 1, features), lambda b: (b, 0, 0))
    down_spec = pl.BlockSpec((1, blocks, rows, features), lambda b: (b, 0, 0, 0))
    flat = whole(hidden.shape)
    return call(
        feed_kernel,
        (blocks,),
        [
            flat,
            flat,
            whole(cot.shape),
            unit_spec(up_weights, lambda b: b),
            down_spec,
            row_spec,
            whole((1, features)),
        ],
        [
            whole((length, width)),
            pl.BlockSpec((fsdp, 1, rows, width), lambda b: (0, b, 0, 0)),
            pl.BlockSpec((1, blocks, rows, width), lambda b: (b, 0, 0, 0)),
            row_spec,
            flat,
        ],
        [
            sds((length, width), BF16),
            sds((fsdp, blocks, rows, width), BF16),
            sds((fsdp, blocks, rows, width), BF16),
            sds((blocks, 1, features), F32),
            sds(hidden.shape, F32),
        ],
        [pltpu.VMEM(hidden.shape, F32)],
    )(hidden, second, cot, up_weights, down_full, up_bias, down_bias)


def store_units(target, made):
    features = made.shape[-1]
    lead = target.shape[:-1]
    target[..., :features] = made.astype(BF16).reshape(lead + (features,))
    target[..., features:] = jnp.zeros(lead + (target.shape[-1] - features,), BF16)


def turn_kernel(second_grad, hidden, cot, attended, weight, gain, stream_grad, att_grad, out_grad, sums):
    features = hidden.shape[-1]
    width = attended.shape[-1]
    normal, inverse = normal_parts(hidden[...])
    upstream = cot[:, :features].astype(F32)
    grad = second_grad[...]
    stream = upstream + normal_pull(normal, inverse, grad * gain[...])
    stream_grad[...] = stream
    low = stream.astype(BF16)
    made = dot(low, square(weight), NT)
    att_grad[:, :features] = made.astype(BF16)
    att_grad[:, features:] = jnp.zeros((hidden.shape[0], width - features), BF16)
    store_units(out_grad, dot(attended[:, :features], low, TN))
    sums[...] = jnp.concatenate(
        [
            jnp.sum(grad * normal, 0, keepdims=True),
            jnp.sum(grad, 0, keepdims=True),
            jnp.sum(low.astype(F32), 0, keepdims=True),
            jnp.sum(upstream, 0, keepdims=True),
            jnp.zeros((4, features), F32),
        ],
        0,
    )


def turn(second_grad, hidden, cot, attended, weights, gain):
    _, features = hidden.shape
    width = attended.shape[-1]
    unit = (weights.shape[1], weights.shape[2], width)
    flat = whole(hidden.shape)
    return call(
        turn_kernel,
        (1,),
        [flat, flat, whole(cot.shape), whole(attended.shape), unit_spec(weights, lambda u: 1), whole((1, features))],
        [flat, whole(attended.shape), whole(unit), whole((8, features))],
        [sds(hidden.shape, F32), sds(attended.shape, BF16), sds(unit, BF16), sds((8, features), F32)],
    )(second_grad, hidden, cot, attended, weights, gain)


def leave_query_kernel(query_grad, first, weight, back, unit_grad, column_sums):
    features = first.shape[-1]
    grad = query_grad[:, :features]
    back[...] = dot(grad, square(weight), NT)
    store_units(unit_grad, dot(first[...], grad, TN))
    column_sums[...] = jnp.sum(grad.astype(F32), 0, keepdims=True)


def leave_query(query_grad, first, weights):
    _, features = first.shape
    unit = (weights.shape[1], weights.shape[2], query_grad.shape[-1])
    return call(
        leave_query_kernel,
        (1,),
        [whole(query_grad.shape), whole(first.shape), unit_spec(weights, lambda u: 0)],
        [whole(first.shape), whole(unit), whole((1, features))],
        [sds(first.shape, F32), sds(unit, BF16), sds((1, features), F32)],
    )(query_grad, first, weights)


def leave_kernel(own, from_core, from_z, first, x, stream_grad, back, weight, gain, token_grad, unit_grad, column_sums, sums, total):
    step = pl.program_id(0)
    features = first.shape[-1]
    summed = own[0, :, :features] + from_core[0, :, :features].astype(F32) + from_z[0, :, :features].astype(F32)
    grad = summed.astype(BF16)
    part = dot(grad, square(weight), NT)
    store_units(unit_grad, dot(first[...], grad, TN))
    column_sums[0] = jnp.sum(grad.astype(F32), 0, keepdims=True)

    @pl.when(step == 0)
    def _():
        total[...] = back[...] + part

    @pl.when(step == 1)
    def _():
        normal, inverse = normal_parts(x[:, :features].astype(F32))
        grad_first = total[...] + part
        low = (stream_grad[...] + normal_pull(normal, inverse, grad_first * gain[...])).astype(BF16)
        token_grad[:, :features] = low
        token_grad[:, features:] = jnp.zeros((low.shape[0], token_grad.shape[1] - features), BF16)
        sums[...] = jnp.concatenate(
            [
                jnp.sum(grad_first * normal, 0, keepdims=True),
                jnp.sum(grad_first, 0, keepdims=True),
                jnp.zeros((6, features), F32),
            ],
            0,
        )


def leave(own, from_core, from_z, first, x, stream_grad, back, weights, gain):
    length, features = first.shape
    width = own.shape[-1]
    unit = (1, weights.shape[1], weights.shape[2], width)
    flat = whole(first.shape)
    kind = pl.BlockSpec((1, length, width), lambda u: (u, 0, 0))
    return call(
        leave_kernel,
        (2,),
        [kind, kind, kind, flat, whole(x.shape), flat, flat, unit_spec(weights, lambda u: u), whole((1, features))],
        [
            whole((length, width)),
            pl.BlockSpec(unit, lambda u: (u, 0, 0, 0)),
            pl.BlockSpec((1, 1, features), lambda u: (u, 0, 0)),
            whole((8, features)),
        ],
        [
            sds((length, width), BF16),
            sds((2,) + unit[1:], BF16),
            sds((2, 1, features), F32),
            sds((8, features), F32),
        ],
        [pltpu.VMEM(first.shape, F32)],
    )(own, from_core, from_z, first, x, stream_grad, back, weights, gain)


def block(
    tokens, w_qkv, qv_bias, w_out, out_bias, w_up, up_bias, w_down, down_bias,
    ln1_gain, ln1_bias, ln2_gain, ln2_bias, cotangent,
):
    _, length, features = tokens.shape
    rows = w_qkv.shape[0]
    half = length // 2
    width = -(-features // LANES) * LANES
    reps = lax.axis_size("rep")
    fsdp = lax.axis_size("fsdp")
    rep_at = lax.axis_index("rep")
    z_at = lax.axis_index("fsdp")
    core = rep_at % 2
    quarter = rep_at // 2 % 4
    grid = ("rep", "fsdp")

    def links(half):
        out = []
        for rep in range(reps):
            for z in range(fsdp):
                to, plane = destination(rep % 2, z, half)
                out.append((rep * fsdp + z, (rep - rep % 2 + to) * fsdp + plane))
        return out

    def flip(bits):
        return [(r * fsdp + z, (r ^ bits) * fsdp + z) for r in range(reps) for z in range(fsdp)]

    def shift(step):
        return [(r * fsdp + z, r * fsdp + (z + step) % fsdp) for r in range(reps) for z in range(fsdp)]

    def flip_z(bits):
        return [(r * fsdp + z, r * fsdp + (z ^ bits)) for r in range(reps) for z in range(fsdp)]

    def turned(perm):
        return [(b, a) for a, b in perm]

    move_a = links(0)
    move_b = links(1)
    to_core = flip(1)
    to_far = flip_z(1)

    def send(value, perm):
        return lax.ppermute(value, grid, perm)

    def swap(value):
        return jnp.concatenate([send(value[:half], move_a), send(value[half:], move_b)], 0)

    def swap_back(value):
        return jnp.concatenate(
            [send(value[:half], turned(move_a)), send(value[half:], turned(move_b))], 0
        )

    def take(value, at, axis=0):
        return lax.dynamic_index_in_dim(value, at, axis, keepdims=False)

    table = lax.dynamic_slice(
        jnp.asarray(task_table()), (core + 2 * (z_at // 2 ^ z_at % 2), 0), (1, 18)
    ).reshape(-1)
    spot = jnp.stack([core, quarter, z_at]).astype(jnp.int32)
    starts = jnp.asarray(CHUNK_STARTS, jnp.int32)

    def gather_group(piece):
        piece = jnp.pad(piece, ((0, 0), (0, 0), (0, width - features)))
        column = jnp.stack([piece] + [send(piece, shift(k)) for k in range(1, fsdp)])
        plane = jnp.stack([column] + [send(column, flip(2 * q)) for q in range(1, 4)])
        return plane, send(plane, to_core)

    def wide_sum(*parts):
        total = parts[0].astype(F32)
        for part in parts[1:]:
            total = total + part.astype(F32)
        return total.astype(BF16)

    def reduce_core(keep, give):
        return wide_sum(keep, send(give, to_core))

    x_at = quarter % 2
    y_at = quarter // 2

    def hold(values, after):
        return values if after is None else lax.optimization_barrier((values, after))[0]

    def stage_plane(total):
        inner = fsdp // 2

        def chunk(value, y, x):
            return lax.dynamic_slice_in_dim(value, starts[2 * y + x], CHUNK, 2)

        left, right = total[:inner], total[inner:]
        got = (
            send(jnp.stack([chunk(left, y, 1 - x_at) for y in range(2)]), flip(2)),
            send(jnp.stack([chunk(right, 1 - y_at, x) for x in range(2)]), flip(4)),
        )
        left = jnp.stack([chunk(left, y, x_at) for y in range(2)])
        right = jnp.stack([chunk(right, y_at, x) for x in range(2)])
        return left, right, got

    def stage_second(state, after=None):
        left, right, got = state
        left_got, right_got = hold(got, after)
        left, right = wide_sum(left, left_got), wide_sum(right, right_got)
        got = (send(take(left, 1 - y_at), flip(4)), send(take(right, 1 - x_at), flip(2)))
        return take(left, y_at), take(right, x_at), got

    def stage_line(state, after=None):
        left, right, got = state
        left_got, right_got = hold(got, after)
        mine = jnp.concatenate([wide_sum(left, left_got), wide_sum(right, right_got)], 0)
        got = tuple(send(take(mine, (z_at + k) % fsdp), shift(k)) for k in range(1, fsdp))
        return take(mine, z_at), got

    def stage_back(state, after=None):
        own, got = state
        own = wide_sum(own, *hold(got, after))
        bit = 8
        while bit < reps:
            own = wide_sum(own, send(own, flip(bit)))
            bit *= 2
        return own, tuple(send(own, flip(2 * q)) for q in range(1, 4))

    def stage_core(state, after=None):
        own, got = state
        four = jnp.stack([own, *hold(got, after)])
        return jnp.stack([four, send(four, to_core)])

    def reduce_small(value):
        value = value + send(value, to_core)
        for part in [send(value, flip(2 * q)) for q in range(1, 4)]:
            value = value + part
        got = [send(take(value, (z_at + k) % fsdp), shift(k)) for k in range(1, fsdp)]
        own = take(value, z_at)
        for part in got:
            own = own + part
        bit = 8
        while bit < reps:
            own = own + send(own, flip(bit))
            bit *= 2
        return own

    lane_pad = ((0, 0), (0, width - features))
    x = swap(jnp.pad(tokens[0], lane_pad))
    cot = swap(jnp.pad(cotangent[0], lane_pad))
    vectors = (qv_bias, out_bias, up_bias, down_bias, ln1_gain, ln1_bias, ln2_gain, ln2_bias)
    mine = jnp.concatenate(vectors)
    column = jnp.stack([mine] + [send(mine, shift(k)) for k in range(1, fsdp)])
    small = jnp.stack([take(column, (z_at - z) % fsdp) for z in range(fsdp)]).astype(F32)
    pieces = []
    start = 0
    for vector in vectors:
        pieces.append(small[:, start : start + vector.shape[0]].reshape(1, -1))
        start += vector.shape[0]
    qv_full, outb_full, upb_full, downb_full, gain_one, shift_one, gain_two, shift_two = pieces

    row_start = starts[quarter]
    kv_piece = lax.dynamic_slice(w_qkv, (row_start, (1 + core) * features), (CHUNK, features))
    query_piece = lax.dynamic_slice(w_qkv, (row_start, 0), (CHUNK, features))
    out_piece = lax.dynamic_slice(w_out, (row_start, 0), (CHUNK, features))
    kv_near, kv_far = gather_group(kv_piece[None])
    kv_weights = assemble(spot, (kv_near, kv_far), rows, features)
    qo_piece = jnp.where(core == 0, query_piece, out_piece)
    qo_weights = assemble(spot, gather_group(qo_piece[None]), rows, features)
    up_piece = jnp.stack(
        [
            lax.dynamic_slice(w_up, (row_start, (2 * g + core) * features), (CHUNK, features))
            for g in range(fsdp // 2)
        ]
    )
    up_weights = assemble(spot, gather_group(up_piece), rows, features)
    down_piece = jnp.stack(
        [
            lax.dynamic_slice(w_down, ((2 * g + core) * rows + row_start, 0), (CHUNK, features))
            for g in range(fsdp // 2)
        ]
    )
    down_full = assemble(spot, gather_group(down_piece), rows, features, by_z=True)

    kv_bias = jnp.stack([jnp.zeros((1, features), F32), qv_full[:, features:]])
    first, pair = enter(x, gain_one, shift_one, kv_weights, kv_bias)
    from_core = send(pair, to_core)
    from_far = send(pair, to_far)
    others = (from_core, from_far, send(from_far, to_core))
    queries = query(first, qo_weights, qv_full[:, :features])
    attended, lse = attention_forward(table, queries, pair, others)
    hidden, second = project(x, attended, qo_weights, outb_full, gain_two, shift_two)
    result, up_grad, down_grad, up_bias_grad, second_grad = feed(
        hidden, second, cot, up_weights, down_full, upb_full.reshape(-1, 1, features), downb_full
    )
    stream_grad, att_grad, out_grad, sums_two = turn(second_grad, hidden, cot, attended, qo_weights, gain_two)
    layer_out = swap_back(result)

    def split_pairs(grad):
        grad = grad.reshape((fsdp, fsdp // 2, 2) + grad.shape[2:])
        return take(grad, core, 2), take(grad, 1 - core, 2)

    up_sum = reduce_core(*split_pairs(up_grad))
    down_sum = reduce_core(*split_pairs(down_grad))
    up_state = stage_plane(up_sum)
    down_state = stage_plane(down_sum)
    dq, *rest = attention_backward(table, queries, pair, others, attended, att_grad, lse)
    own_pair, core_pair, far_pair, last_pair = rest
    far_sum = wide_sum(far_pair, send(last_pair, to_core))
    far_got = send(far_sum, to_far)
    core_got = send(core_pair, to_core)
    back, query_grad, query_sums = leave_query(dq, first, qo_weights)
    up_state = stage_second(up_state, far_sum)
    down_state = stage_second(down_state, far_sum)
    qo_sum = reduce_core(
        jnp.where(core == 0, query_grad, out_grad)[:, None],
        jnp.where(core == 0, out_grad, query_grad)[:, None],
    )
    qo_state = stage_plane(qo_sum)
    up_state = stage_line(up_state, query_grad)
    down_state = stage_line(down_state, query_grad)
    token_low, kv_grad, column_sums, sums_one = leave(
        own_pair, core_got, far_got, first, x, stream_grad, back, kv_weights, gain_one
    )
    kv_sum = reduce_core(take(kv_grad, core)[:, None], take(kv_grad, 1 - core)[:, None])
    qo_state = stage_second(qo_state, token_low)
    kv_state = stage_plane(kv_sum)
    kv_state = stage_second(kv_state)
    up_state = stage_back(up_state, kv_state[0])
    down_state = stage_back(down_state, kv_state[0])
    kv_state = stage_line(kv_state)
    line_done = kv_state[0]
    qo_state = stage_line(qo_state, line_done)
    kv_state = stage_back(kv_state)
    up_group = stage_core(up_state, kv_state[0])
    down_group = stage_core(down_state, kv_state[0])
    qo_state = stage_back(qo_state, kv_state[0])
    kv_group = stage_core(kv_state)
    qo_group = stage_core(qo_state)
    grad_tokens = hold(swap_back(token_low), line_done)[:, :features].astype(F32)
    layer_out = hold(layer_out, line_done)[:, :features].astype(F32)
    vectors = (
        sums_two[2], up_bias_grad, sums_two[3], sums_two[0], sums_two[1],
        jnp.concatenate([query_sums, column_sums[1]], 1), sums_one[0], sums_one[1],
    )
    own_row = reduce_small(jnp.concatenate([v.reshape(fsdp, -1) for v in vectors], 1))
    small_own = []
    start = 0
    for v in vectors:
        size = v.size // fsdp
        small_own.append(own_row[start : start + size])
        start += size
    out_b, up_b, down_b, gain_two_g, shift_two_g, qv_b, gain_one_g, shift_one_g = small_own
    beside = [(0, b * features, features) for b in range(fsdp)]
    below = [(b * rows, 0, features) for b in range(fsdp)]
    (up_own,) = finish(spot, [up_group], [(rows, fsdp * features)], [(0, 0, 0, 0)], [beside])
    (down_own,) = finish(spot, [down_group], [(features, features)], [(0, 0, 0, 0)], [below])
    qkv_own, out_own = finish(
        spot,
        [qo_group, kv_group],
        [(rows, 3 * features), (rows, features)],
        [(0, 1), (0, 0)],
        [[beside[0], beside[0]], beside[1:3]],
    )
    return (
        layer_out[None], grad_tokens[None],
        qkv_own, qv_b, out_own, out_b,
        up_own, up_b, down_own, down_b,
        gain_one_g, shift_one_g, gain_two_g, shift_two_g,
    )


def solution(mesh):
    data = P("rep", "fsdp", None)
    matrix = P("fsdp", None)
    vector = P("fsdp")
    return jax.shard_map(
        block,
        mesh=mesh,
        in_specs=(
            data, matrix, vector, matrix, vector, matrix, vector, matrix, vector,
            vector, vector, vector, vector, data,
        ),
        out_specs=(
            data, data, matrix, vector, matrix, vector, matrix, vector, matrix, vector,
            vector, vector, vector, vector,
        ),
        check_vma=False,
    )
```

time: 946 us -> 902 us (0.953)
  waiting for transfers between devices: 566 us -> 356 us
  starting transfers between devices: 32.5 us -> 170 us
  blocking collectives: 99.2 us -> 0 us
  other arithmetic: 29.1 us -> 83.7 us
  Pallas kernels: 162 us -> 207 us
  local copies, waits for them, and re-layouts: 40.3 us -> 55.4 us
    unnamed x12 -> x0, waiting for transfers between devices: 283 us -> none
    ppermute x14 -> x100, waiting for transfers between devices: 206 us -> 356 us  [send(): return lax.ppermute(value, grid, perm)]
    ppermute x14 -> x100, starting transfers between devices: 32.1 us -> 170 us  [send(): return lax.ppermute(value, grid, perm)]
    all_gather x6 -> x0, waiting for transfers between devices: 77.2 us -> none  [the longest x3 77.2 us: gather_all(): return lax.all_gather(own_piece(matrix), everyone, axis=0, tiled=True)]
    psum x1 -> x0, blocking collectives: 61.6 us -> none  [local(): stacked = lax.psum(stacked, grid)]
    pallas_call x7 -> x16, Pallas kernels: 162 us -> 207 us  [the longest x1 50.5 us: feed(): call(feed_kernel, (blocks,), [flat, flat, whole(cot.shape), unit_spec(up_...]
    another operation x3 -> x29, other arithmetic: 2.93 us -> 46.2 us  [the longest x8 21.6 us: gather_group(): jnp.stack([column] + [send(column, flip(2 * q)) for q in range(1, 4)])]
    unnamed x1 -> x0, blocking collectives: 37.7 us -> none
  transfers between devices with their start and end apart: 23 -> 100, of which waited for: 11 -> 43; matrix products, arithmetic and copies ran while one was open for 6% -> 14% of each run, Pallas kernels for 10% -> 8%
where the time goes in v3:
time: 902 us; the launch traced here: 892 us
  waiting for transfers between devices  356 us (39%)
  Pallas kernels  207 us (23%)
  starting transfers between devices  170 us (19%)
  other arithmetic  83.7 us (9%)
  local copies, waits for them, and re-layouts  55.4 us (6%)
  between operations  20.6 us (2%)
    ppermute x100, waiting for transfers between devices, send(): return lax.ppermute(value, grid, perm)  356 us
    ppermute x100, starting transfers between devices, send(): return lax.ppermute(value, grid, perm)  170 us
    pallas_call x1, Pallas kernels, feed(): call(feed_kernel, (blocks,), [flat, flat, whole(cot.shape), unit_spec(up_...  50.5 us
    pallas_call x1, Pallas kernels, attention_backward(): call(attend_backward, (pairs,), specs + [flat, flat, pl.BlockSpec((1, 2,...  34.8 us
    pallas_call x4, Pallas kernels, assemble(): call(functools.partial(assemble_kernel, by_z=by_z), (units,), [pl.BlockSp...  32 us
    convert_element_type x25, other arithmetic, wide_sum(): return total.astype(BF16)  29.4 us
    pallas_call x1, Pallas kernels, attention_forward(): call(attend_forward, (pairs,), specs, [pl.BlockSpec((length, LANES), lamb...  21.9 us
    another operation x8, other arithmetic, gather_group(): jnp.stack([column] + [send(column, flip(2 * q)) for q in range(1, 4)])  21.6 us
  transfers between devices with their start and end apart: 100, of which 43 were waited for; matrix products, arithmetic and copies ran while one was open for 14% of the time, Pallas kernels for 8%

profile of v3, /device:TPU:0, one launch (start us, length us, event | category | flops | bytes accessed | tf_op | source)
XLA Modules:
  0.0 892.3 jit_solution(15631171301762357385)
XLA Ops:
  55.4 17.3 %collective-permute-done.25 = bf16[2,72,1152]{2,1,0:T(8,128)(2,1)S(1)} collective-permute-done((bf16[2,72,1152]{2,1,0:T(8,128)(2,1)S(1)}, bf16[2,72,1152]{2,1,0:T(8,128)(2,1)S(1)}, u32[]{:S(2)}, u32[]{:S(2)}) %collective-permute-start.25) | collective-permute-done | bytes 331808 | tf_op jit(solution)/shard_map/ppermute | solution.py:677
  77.6 9.3 %collective-permute-done.32 = bf16[2,72,1152]{2,1,0:T(8,128)(2,1)S(1)} collective-permute-done((bf16[2,72,1152]{2,1,0:T(8,128)(2,1)S(1)}, bf16[2,72,1152]{2,1,0:T(8,128)(2,1)S(1)}, u32[]{:S(2)}, u32[]{:S(2)}) %collective-permute-start.32) | collective-permute-done | bytes 331808 | tf_op jit(solution)/shard_map/ppermute | solution.py:677
  92.8 23.2 %collective-permute-done.8 = bf16[4,1,72,1152]{3,2,0,1:T(8,128)(2,1)S(1)} collective-permute-done((bf16[4,1,72,1152]{3,2,0,1:T(8,128)(2,1)S(1)}, bf16[4,1,72,1152]{3,2,0,1:T(8,128)(2,1)S(1)}, u32[]{:S(2)}, u32[]{:S(2)}) %collective-permute-start.8) | collective-permute-done | bytes 663584 | tf_op jit(solution)/shard_map/ppermute | solution.py:677
  117.5 13.8 %collective-permute-done.10 = bf16[4,1,72,1152]{3,2,0,1:T(8,128)(2,1)S(1)} collective-permute-done((bf16[4,1,72,1152]{3,2,0,1:T(8,128)(2,1)S(1)}, bf16[4,1,72,1152]{3,2,0,1:T(8,128)(2,1)S(1)}, u32[]{:S(2)}, u32[]{:S(2)}) %collective-permute-start.10) | collective-permute-done | bytes 663584 | tf_op jit(solution)/shard_map/ppermute | solution.py:677
  135.9 23.8 %collective-permute-done.29 = bf16[4,2,72,1152]{3,2,1,0:T(8,128)(2,1)} collective-permute-done((bf16[4,2,72,1152]{3,2,1,0:T(8,128)(2,1)}, bf16[4,2,72,1152]{3,2,1,0:T(8,128)(2,1)}, u32[]{:S(2)}, u32[]{:S(2)}) %collective-permute-start.29) | collective-permute-done | bytes 1327136 | tf_op jit(solution)/shard_map/ppermute | solution.py:677
  165.1 9.5 %collective-permute-done.35 = bf16[4,2,72,1152]{3,2,1,0:T(8,128)(2,1)} collective-permute-done((bf16[4,2,72,1152]{3,2,1,0:T(8,128)(2,1)}, bf16[4,2,72,1152]{3,2,1,0:T(8,128)(2,1)}, u32[]{:S(2)}, u32[]{:S(2)}) %collective-permute-start.35) | collective-permute-done | bytes 1327136 | tf_op jit(solution)/shard_map/ppermute | solution.py:677
  176.4 10.9 %collective-permute-done.34 = bf16[4,2,72,1152]{3,2,1,0:T(8,128)(2,1)} collective-permute-done((bf16[4,2,72,1152]{3,2,1,0:T(8,128)(2,1)}, bf16[4,2,72,1152]{3,2,1,0:T(8,128)(2,1)}, u32[]{:S(2)}, u32[]{:S(2)}) %collective-permute-start.34) | collective-permute-done | bytes 1327136 | tf_op jit(solution)/shard_map/ppermute | solution.py:677
  187.2 16.6 %collective-permute-start.30 = (bf16[4,4,2,72,1152]{4,3,2,1,0:T(8,128)(2,1)}, bf16[4,4,2,72,1152]{4,3,2,1,0:T(8,128)(2,1)}, u32[]{:S(2)}, u32[]{:S(2)}) collective-permute-start(bf16[4,4,2,72,1152]{4,3,2,1,0:T(8,128)(2,1)} %pad_maximum_fusion.near), channel_id=1, source_target_pairs={{0,4},{1,5},{2,6},{3,7},{4,0},{5,1},{6,2},{7,3},{8,12},{9,13},{10,... | collective-permute-start | bytes 15925256 | tf_op jit(solution)/shard_map/ppermute | solution.py:677
  216.3 24.6 %collective-permute-start.13 = (bf16[1,72,1152]{2,1,0:T(8,128)(2,1)S(1)}, bf16[1,72,1152]{2,1,0:T(8,128)(2,1)S(1)}, u32[]{:S(2)}, u32[]{:S(2)}) collective-permute-start(bf16[1,72,1152]{2,1,0:T(8,128)(2,1)S(1)} %get-tuple-element.245), channel_id=1, source_target_pairs={{0,2},{1,3},{2,0},{3,1},{4,6},{5,7},{6,4},{7,5},{8,10},{9,11},{10,... | collective-permute-start | bytes 497672 | tf_op jit(solution)/shard_map/ppermute | solution.py:677
  264.1 14.7 %collective-permute-done.16 = bf16[4,1,72,1152]{3,2,0,1:T(8,128)(2,1)S(1)} collective-permute-done((bf16[4,1,72,1152]{3,2,0,1:T(8,128)(2,1)}, bf16[4,1,72,1152]{3,2,0,1:T(8,128)(2,1)S(1)}, u32[]{:S(2)}, u32[]{:S(2)}) %collective-permute-start.16) | collective-permute-done | bytes 663584 | tf_op jit(solution)/shard_map/ppermute | solution.py:677
  281.9 14.6 %collective-permute-done.17 = bf16[4,1,72,1152]{3,2,0,1:T(8,128)(2,1)} collective-permute-done((bf16[4,1,72,1152]{3,2,0,1:T(8,128)(2,1)}, bf16[4,1,72,1152]{3,2,0,1:T(8,128)(2,1)}, u32[]{:S(2)}, u32[]{:S(2)}) %collective-permute-start.17) | collective-permute-done | bytes 663584 | tf_op jit(solution)/shard_map/ppermute | solution.py:677
  301.7 15.9 %collective-permute-done.23 = bf16[256,1152]{1,0:T(8,128)(2,1)S(1)} collective-permute-done((bf16[256,1152]{1,0:T(8,128)(2,1)S(1)}, bf16[256,1152]{1,0:T(8,128)(2,1)S(1)}, u32[]{:S(2)}, u32[]{:S(2)}) %collective-permute-start.23) | collective-permute-done | bytes 589856 | tf_op jit(solution)/shard_map/ppermute | solution.py:677
  341.8 10.3 %shard_map.269.up = bf16[4,4,272,1088]{3,2,1,0:T(8,128)(2,1)} custom-call(s32[3]{0:T(128)} %pad_add_fusion.spot, bf16[4,4,2,72,1152]{4,3,2,1,0:T(8,128)(2,1)} %pad_maximum_fusion.near, bf16[4,4,2,72,1152]{4,3,2,1,0:T(8,128)(2,1)} %collective-permute-done.30.far), custom_call_target="tpu_custom_call" | custom-call | tf_op jit(solution)/shard_map/pallas_call | solution.py:328
  352.2 10.3 %shard_map.270.down = bf16[4,4,272,1088]{3,2,1,0:T(8,128)(2,1)} custom-call(s32[3]{0:T(128)} %pad_add_fusion.spot, bf16[4,4,2,72,1152]{4,3,2,1,0:T(8,128)(2,1)} %pad_maximum_fusion.1.near, bf16[4,4,2,72,1152]{4,3,2,1,0:T(8,128)(2,1)} %collective-permute-done.37.far), custom_call_target="tpu_custom_call" | custom-call | tf_op jit(solution)/shard_map/pallas_call | solution.py:328
  362.5 21.9 %shard_map.267 = (bf16[512,1152]{1,0:T(8,128)(2,1)}, f32[9,2,1,512]{3,2,1,0:T(1,128)}) custom-call(s32[18]{0:T(128)} %fusion.62.tab, bf16[512,1152]{1,0:T(8,128)(2,1)} %shard_map.266.q, bf16[2,512,1152]{2,1,0:T(8,128)(2,1)} %get-tuple-element.73.k0.v0, bf16[2,512,1152]{2,1,0:T(8,128)(2,1)} %collective-permute-done.19.k1.v1, ...), custom_call_target="tpu_custom_call" | custom-call | tf_op jit(solution)/shard_map/pallas_call | solution.py:227
  390.5 50.5 %shard_map.271 = (bf16[512,1152]{1,0:T(8,128)(2,1)}, bf16[4,4,272,1152]{3,2,1,0:T(8,128)(2,1)}, bf16[4,4,272,1152]{3,2,1,0:T(8,128)(2,1)}, f32[4,1,1088]{2,1,0:T(1,128)}, f32[512,1088]{1,0:T(8,128)}) custom-call(f32[512,1088]{1,0:T(8,128)} %get-tuple-element.75.hidden, bf16[512,1088]{1,0:T(8,128)(2,1)} %get-tuple-element.76.second, ...), custom_call_target="tpu_custom_call" | custom-call | tf_op jit(solution)/shard_map/pallas_call | solution.py:483
  441.0 10.0 %shard_map.272 = (f32[512,1088]{1,0:T(8,128)}, bf16[512,1152]{1,0:T(8,128)(2,1)}, bf16[4,272,1152]{2,1,0:T(8,128)(2,1)}, f32[8,1088]{1,0:T(8,128)}) custom-call(f32[512,1088]{1,0:T(8,128)} %get-tuple-element.78.second_grad, f32[512,1088]{1,0:T(8,128)} %get-tuple-element.75.hidden, bf16[512,1152]{1,0:T(8,128)(2,1)} %copy-done.4, ...), custom_call_target="tpu_custom_call" | custom-call | tf_op jit(solution)/shard_map/pallas_call | solution.py:550
  451.0 34.8 %shard_map.273 = (bf16[512,1152]{1,0:T(8,128)(2,1)}, f32[2,512,1152]{2,1,0:T(8,128)}, bf16[2,512,1152]{2,1,0:T(8,128)(2,1)}, bf16[2,512,1152]{2,1,0:T(8,128)(2,1)}, bf16[2,512,1152]{2,1,0:T(8,128)(2,1)}) custom-call(s32[18]{0:T(128)} %fusion.62.tab, bf16[512,1152]{1,0:T(8,128)(2,1)} %shard_map.266.q, bf16[2,512,1152]{2,1,0:T(8,128)(2,1)} %get-tuple-element.73.k0.v0, ...), custom_call_target="tpu_custom_call" | custom-call | tf_op jit(solution)/shard_map/pallas_call | solution.py:253
  543.9 45.3 %collective-permute-done.42.from_z = bf16[2,512,1152]{2,1,0:T(8,128)(2,1)} collective-permute-done((bf16[2,512,1152]{2,1,0:T(8,128)(2,1)S(1)}, bf16[2,512,1152]{2,1,0:T(8,128)(2,1)}, u32[]{:S(2)}, u32[]{:S(2)}) %collective-permute-start.42) | collective-permute-done | bytes 2359328 | tf_op jit(solution)/shard_map/ppermute | solution.py:677
  589.3 16.6 %shard_map.275 = (bf16[512,1152]{1,0:T(8,128)(2,1)}, bf16[2,4,272,1152]{3,2,1,0:T(8,128)(2,1)}, f32[2,1,1088]{2,1,0:T(1,128)}, f32[8,1088]{1,0:T(8,128)}) custom-call(f32[2,512,1152]{2,1,0:T(8,128)} %get-tuple-element.81.own, bf16[2,512,1152]{2,1,0:T(8,128)(2,1)} %collective-permute-done.40.from_core, bf16[2,512,1152]{2,1,0:T(8,128)(2,1)} %collective-permute-done.42.from_z, ...), custom_call_target="tpu_custom_call" | custom-call | tf_op jit(solution)/shard_map/pallas_call | solution.py:615
  658.4 18.3 %collective-permute-done.90 = bf16[2,2,2,72,1152]{4,3,2,1,0:T(8,128)(2,1)} collective-permute-done((bf16[2,2,2,72,1152]{4,3,2,1,0:T(8,128)(2,1)}, bf16[2,2,2,72,1152]{4,3,2,1,0:T(8,128)(2,1)}, u32[]{:S(2)}, u32[]{:S(2)}) %collective-permute-start.90) | collective-permute-done | bytes 1327136 | tf_op jit(solution)/shard_map/ppermute | solution.py:677
  685.3 19.7 %collective-permute-done.78 = bf16[2,2,2,72,1152]{4,3,2,1,0:T(8,128)(2,1)S(1)} collective-permute-done((bf16[2,2,2,72,1152]{4,3,2,1,0:T(8,128)(2,1)S(1)}, bf16[2,2,2,72,1152]{4,3,2,1,0:T(8,128)(2,1)S(1)}, u32[]{:S(2)}, u32[]{:S(2)}) %collective-permute-start.78) | collective-permute-done | bytes 1327136 | tf_op jit(solution)/shard_map/ppermute | solution.py:677
  740.1 14.2 %collective-permute-done.44 = bf16[2,2,1,72,1152]{4,3,1,2,0:T(8,128)(2,1)S(1)} collective-permute-done((bf16[2,2,1,72,1152]{4,3,1,2,0:T(8,128)(2,1)S(1)}, bf16[2,2,1,72,1152]{4,3,1,2,0:T(8,128)(2,1)S(1)}, u32[]{:S(2)}, u32[]{:S(2)}) %collective-permute-start.44) | collective-permute-done | bytes 663584 | tf_op jit(solution)/shard_map/ppermute | solution.py:677
  756.0 13.3 %collective-permute-done.46 = bf16[2,2,1,72,1152]{4,3,1,2,0:T(8,128)(2,1)S(1)} collective-permute-done((bf16[2,2,1,72,1152]{4,3,1,2,0:T(8,128)(2,1)S(1)}, bf16[2,2,1,72,1152]{4,3,1,2,0:T(8,128)(2,1)S(1)}, u32[]{:S(2)}, u32[]{:S(2)}) %collective-permute-start.46) | collective-permute-done | bytes 663584 | tf_op jit(solution)/shard_map/ppermute | solution.py:677
  (430 shorter events, 412.3 us)
Async XLA Ops:
  75.5 59.2 %collective-permute-start.28 = (bf16[4,2,72,1152]{3,2,1,0:T(8,128)(2,1)}, bf16[4,2,72,1152]{3,2,1,0:T(8,128)(2,1)}, u32[]{:S(2)}, u32[]{:S(2)}) collective-permute-start(bf16[4,2,72,1152]{3,2,1,0:T(8,128)(2,1)} %get-tuple-element.201), channel_id=1, source_target_pairs={{0,16},{1,17},{2,18},{3,19},{4,20},{5,21},{6,22},{7,23},{8,24},{9,... | collective-permute-start | bytes 3981320 | tf_op jit(solution)/shard_map/ppermute | solution.py:677
  76.0 59.1 %collective-permute-start.27 = (bf16[4,2,72,1152]{3,2,1,0:T(8,128)(2,1)}, bf16[4,2,72,1152]{3,2,1,0:T(8,128)(2,1)}, u32[]{:S(2)}, u32[]{:S(2)}) collective-permute-start(bf16[4,2,72,1152]{3,2,1,0:T(8,128)(2,1)} %get-tuple-element.201), channel_id=1, source_target_pairs={{0,8},{1,9},{2,10},{3,11},{4,12},{5,13},{6,14},{7,15},{8,0},{9,1},... | collective-permute-start | bytes 3981320 | tf_op jit(solution)/shard_map/ppermute | solution.py:677
  90.0 69.8 %collective-permute-start.29 = (bf16[4,2,72,1152]{3,2,1,0:T(8,128)(2,1)}, bf16[4,2,72,1152]{3,2,1,0:T(8,128)(2,1)}, u32[]{:S(2)}, u32[]{:S(2)}) collective-permute-start(bf16[4,2,72,1152]{3,2,1,0:T(8,128)(2,1)} %get-tuple-element.201), channel_id=1, source_target_pairs={{0,24},{1,25},{2,26},{3,27},{4,28},{5,29},{6,30},{7,31},{8,16},{9,... | collective-permute-start | bytes 3981320 | tf_op jit(solution)/shard_map/ppermute | solution.py:677
  116.0 58.7 %collective-permute-start.35 = (bf16[4,2,72,1152]{3,2,1,0:T(8,128)(2,1)}, bf16[4,2,72,1152]{3,2,1,0:T(8,128)(2,1)}, u32[]{:S(2)}, u32[]{:S(2)}) collective-permute-start(bf16[4,2,72,1152]{3,2,1,0:T(8,128)(2,1)} %get-tuple-element.199), channel_id=1, source_target_pairs={{0,16},{1,17},{2,18},{3,19},{4,20},{5,21},{6,22},{7,23},{8,24},{9,... | collective-permute-start | bytes 3981320 | tf_op jit(solution)/shard_map/ppermute | solution.py:677
  131.3 56.0 %collective-permute-start.34 = (bf16[4,2,72,1152]{3,2,1,0:T(8,128)(2,1)}, bf16[4,2,72,1152]{3,2,1,0:T(8,128)(2,1)}, u32[]{:S(2)}, u32[]{:S(2)}) collective-permute-start(bf16[4,2,72,1152]{3,2,1,0:T(8,128)(2,1)} %get-tuple-element.199), channel_id=1, source_target_pairs={{0,8},{1,9},{2,10},{3,11},{4,12},{5,13},{6,14},{7,15},{8,0},{9,1},... | collective-permute-start | bytes 3981320 | tf_op jit(solution)/shard_map/ppermute | solution.py:677
  134.7 74.2 %collective-permute-start.36 = (bf16[4,2,72,1152]{3,2,1,0:T(8,128)(2,1)}, bf16[4,2,72,1152]{3,2,1,0:T(8,128)(2,1)}, u32[]{:S(2)}, u32[]{:S(2)}) collective-permute-start(bf16[4,2,72,1152]{3,2,1,0:T(8,128)(2,1)} %get-tuple-element.199), channel_id=1, source_target_pairs={{0,24},{1,25},{2,26},{3,27},{4,28},{5,29},{6,30},{7,31},{8,16},{9,... | collective-permute-start | bytes 3981320 | tf_op jit(solution)/shard_map/ppermute | solution.py:677
  135.1 106.0 %collective-permute-start.11 = (bf16[4,4,1,72,1152]{4,3,2,1,0:T(8,128)(2,1)}, bf16[4,4,1,72,1152]{4,3,2,1,0:T(8,128)(2,1)}, u32[]{:S(2)}, u32[]{:S(2)}) collective-permute-start(bf16[4,4,1,72,1152]{4,3,2,1,0:T(8,128)(2,1)} %pad_maximum_fusion.2.near), channel_id=1, source_target_pairs={{0,4},{1,5},{2,6},{3,7},{4,0},{5,1},{6,2},{7,3},{8,12},{9,13},{10,... | collective-permute-start | bytes 7962632 | tf_op jit(solution)/shard_map/ppermute | solution.py:677
  159.8 81.3 %collective-permute-start.1 = (bf16[256,1152]{1,0:T(8,128)(2,1)}, bf16[256,1152]{1,0:T(8,128)(2,1)}, u32[]{:S(2)}, u32[]{:S(2)}) collective-permute-start(bf16[256,1152]{1,0:T(8,128)(2,1)} %get-tuple-element.224), channel_id=1, source_target_pairs={{0,4},{1,5},{2,1},{3,0},{4,7},{5,6},{6,2},{7,3},{8,12},{9,13},{10,... | collective-permute-start | bytes 1769480 | tf_op jit(solution)/shard_map/ppermute | solution.py:677
  187.2 154.6 %collective-permute-start.30 = (bf16[4,4,2,72,1152]{4,3,2,1,0:T(8,128)(2,1)}, bf16[4,4,2,72,1152]{4,3,2,1,0:T(8,128)(2,1)}, u32[]{:S(2)}, u32[]{:S(2)}) collective-permute-start(bf16[4,4,2,72,1152]{4,3,2,1,0:T(8,128)(2,1)} %pad_maximum_fusion.near), channel_id=1, source_target_pairs={{0,4},{1,5},{2,6},{3,7},{4,0},{5,1},{6,2},{7,3},{8,12},{9,13},{10,... | collective-permute-start | bytes 15925256 | tf_op jit(solution)/shard_map/ppermute | solution.py:677
  214.3 137.9 %collective-permute-start.37 = (bf16[4,4,2,72,1152]{4,3,2,1,0:T(8,128)(2,1)}, bf16[4,4,2,72,1152]{4,3,2,1,0:T(8,128)(2,1)}, u32[]{:S(2)}, u32[]{:S(2)}) collective-permute-start(bf16[4,4,2,72,1152]{4,3,2,1,0:T(8,128)(2,1)} %pad_maximum_fusion.1.near), channel_id=1, source_target_pairs={{0,4},{1,5},{2,6},{3,7},{4,0},{5,1},{6,2},{7,3},{8,12},{9,13},{10,... | collective-permute-start | bytes 15925256 | tf_op jit(solution)/shard_map/ppermute | solution.py:677
  259.5 65.8 %collective-permute-start.20 = (bf16[2,512,1152]{2,1,0:T(8,128)(2,1)}, bf16[2,512,1152]{2,1,0:T(8,128)(2,1)}, u32[]{:S(2)}, u32[]{:S(2)}) collective-permute-start(bf16[2,512,1152]{2,1,0:T(8,128)(2,1)} %get-tuple-element.73.k0.v0), channel_id=1, source_target_pairs={{0,1},{1,0},{2,3},{3,2},{4,5},{5,4},{6,7},{7,6},{8,9},{9,8},{10,11... | collective-permute-start | bytes 7077896 | tf_op jit(solution)/shard_map/ppermute | solution.py:677
  317.6 44.9 %collective-permute-start.19 = (bf16[2,512,1152]{2,1,0:T(8,128)(2,1)S(1)}, bf16[2,512,1152]{2,1,0:T(8,128)(2,1)}, u32[]{:S(2)}, u32[]{:S(2)}) collective-permute-start(bf16[2,512,1152]{2,1,0:T(8,128)(2,1)S(1)} %copy-done), channel_id=1, source_target_pairs={{0,4},{1,5},{2,6},{3,7},{4,0},{5,1},{6,2},{7,3},{8,12},{9,13},{10,... | collective-permute-start | bytes 7077896 | tf_op jit(solution)/shard_map/ppermute | solution.py:677
  533.0 103.2 %collective-permute-start.88 = (bf16[4,2,272,1152]{3,2,1,0:T(8,128)(2,1)}, bf16[4,2,272,1152]{3,2,1,0:T(8,128)(2,1)}, u32[]{:S(2)}, u32[]{:S(2)}) collective-permute-start(bf16[4,2,272,1152]{3,2,1,0:T(8,128)(2,1)} %dynamic-slice_bitcast_fusion), channel_id=1, source_target_pairs={{0,4},{1,5},{2,6},{3,7},{4,0},{5,1},{6,2},{7,3},{8,12},{9,13},{10,... | collective-permute-start | bytes 15040520 | tf_op jit(solution)/shard_map/ppermute | solution.py:677
  535.9 53.3 %collective-permute-start.42 = (bf16[2,512,1152]{2,1,0:T(8,128)(2,1)S(1)}, bf16[2,512,1152]{2,1,0:T(8,128)(2,1)}, u32[]{:S(2)}, u32[]{:S(2)}) collective-permute-start(bf16[2,512,1152]{2,1,0:T(8,128)(2,1)S(1)} %add_convert_fusion), channel_id=1, source_target_pairs={{0,1},{1,0},{2,3},{3,2},{4,5},{5,4},{6,7},{7,6},{8,9},{9,8},{10,11... | collective-permute-start | bytes 7077896 | tf_op jit(solution)/shard_map/ppermute | solution.py:677
  540.2 67.8 %collective-permute-start.52 = (bf16[2,2,1,72,1152]{4,3,1,2,0:T(8,128)(2,1)}, bf16[2,2,1,72,1152]{4,3,1,2,0:T(8,128)(2,1)}, u32[]{:S(2)}, u32[]{:S(2)}) collective-permute-start(bf16[2,2,1,72,1152]{4,3,1,2,0:T(8,128)(2,1)} %pad_maximum_fusion.23), channel_id=1, source_target_pairs={{0,16},{1,17},{2,18},{3,19},{4,20},{5,21},{6,22},{7,23},{8,24},{9,... | collective-permute-start | bytes 1990664 | tf_op jit(solution)/shard_map/ppermute | solution.py:677
  541.0 67.0 %collective-permute-start.51 = (bf16[2,2,1,72,1152]{4,3,1,2,0:T(8,128)(2,1)S(1)}, bf16[2,2,1,72,1152]{4,3,1,2,0:T(8,128)(2,1)}, u32[]{:S(2)}, u32[]{:S(2)}) collective-permute-start(bf16[2,2,1,72,1152]{4,3,1,2,0:T(8,128)(2,1)S(1)} %pad_maximum_fusion.22), channel_id=1, source_target_pairs={{0,8},{1,9},{2,10},{3,11},{4,12},{5,13},{6,14},{7,15},{8,0},{9,1},... | collective-permute-start | bytes 1990664 | tf_op jit(solution)/shard_map/ppermute | solution.py:677
  543.9 103.5 %collective-permute-start.76 = (bf16[4,2,272,1152]{3,2,1,0:T(8,128)(2,1)}, bf16[4,2,272,1152]{3,2,1,0:T(8,128)(2,1)}, u32[]{:S(2)}, u32[]{:S(2)}) collective-permute-start(bf16[4,2,272,1152]{3,2,1,0:T(8,128)(2,1)} %dynamic-slice_bitcast_fusion.1), channel_id=1, source_target_pairs={{0,4},{1,5},{2,6},{3,7},{4,0},{5,1},{6,2},{7,3},{8,12},{9,13},{10,... | collective-permute-start | bytes 15040520 | tf_op jit(solution)/shard_map/ppermute | solution.py:677
  633.8 101.9 %collective-permute-start.43 = (bf16[4,1,272,1152]{3,2,0,1:T(8,128)(2,1)}, bf16[4,1,272,1152]{3,2,0,1:T(8,128)(2,1)}, u32[]{:S(2)}, u32[]{:S(2)}) collective-permute-start(bf16[4,1,272,1152]{3,2,0,1:T(8,128)(2,1)} %dynamic-slice_bitcast_fusion.2), channel_id=1, source_target_pairs={{0,4},{1,5},{2,6},{3,7},{4,0},{5,1},{6,2},{7,3},{8,12},{9,13},{10,... | collective-permute-start | bytes 7520264 | tf_op jit(solution)/shard_map/ppermute | solution.py:677
  653.3 51.7 %collective-permute-start.78 = (bf16[2,2,2,72,1152]{4,3,2,1,0:T(8,128)(2,1)S(1)}, bf16[2,2,2,72,1152]{4,3,2,1,0:T(8,128)(2,1)S(1)}, u32[]{:S(2)}, u32[]{:S(2)}) collective-permute-start(bf16[2,2,2,72,1152]{4,3,2,1,0:T(8,128)(2,1)S(1)} %pad_maximum_fusion.11), channel_id=1, source_target_pairs={{0,16},{1,17},{2,18},{3,19},{4,20},{5,21},{6,22},{7,23},{8,24},{9,... | collective-permute-start | bytes 3981320 | tf_op jit(solution)/shard_map/ppermute | solution.py:677
  654.5 53.5 %collective-permute-start.77 = (bf16[2,2,2,72,1152]{4,3,2,1,0:T(8,128)(2,1)S(1)}, bf16[2,2,2,72,1152]{4,3,2,1,0:T(8,128)(2,1)S(1)}, u32[]{:S(2)}, u32[]{:S(2)}) collective-permute-start(bf16[2,2,2,72,1152]{4,3,2,1,0:T(8,128)(2,1)S(1)} %pad_maximum_fusion.10), channel_id=1, source_target_pairs={{0,8},{1,9},{2,10},{3,11},{4,12},{5,13},{6,14},{7,15},{8,0},{9,1},... | collective-permute-start | bytes 3981320 | tf_op jit(solution)/shard_map/ppermute | solution.py:677
  723.1 54.4 %collective-permute-start.95 = (bf16[2,72,1152]{2,1,0:T(8,128)(2,1)S(1)}, bf16[2,72,1152]{2,1,0:T(8,128)(2,1)S(1)}, u32[]{:S(2)}, u32[]{:S(2)}) collective-permute-start(bf16[2,72,1152]{2,1,0:T(8,128)(2,1)S(1)} %get-tuple-element.190), channel_id=1, source_target_pairs={{0,3},{1,0},{2,1},{3,2},{4,7},{5,4},{6,5},{7,6},{8,11},{9,8},{10,9... | collective-permute-start | bytes 995336 | tf_op jit(solution)/shard_map/ppermute | solution.py:677
  723.3 61.1 %collective-permute-start.93 = (bf16[2,72,1152]{2,1,0:T(8,128)(2,1)S(1)}, bf16[2,72,1152]{2,1,0:T(8,128)(2,1)S(1)}, u32[]{:S(2)}, u32[]{:S(2)}) collective-permute-start(bf16[2,72,1152]{2,1,0:T(8,128)(2,1)S(1)} %get-tuple-element.191), channel_id=1, source_target_pairs={{0,1},{1,2},{2,3},{3,0},{4,5},{5,6},{6,7},{7,4},{8,9},{9,10},{10,1... | collective-permute-start | bytes 995336 | tf_op jit(solution)/shard_map/ppermute | solution.py:677
  732.5 54.1 %collective-permute-start.94 = (bf16[2,72,1152]{2,1,0:T(8,128)(2,1)S(1)}, bf16[2,72,1152]{2,1,0:T(8,128)(2,1)S(1)}, u32[]{:S(2)}, u32[]{:S(2)}) collective-permute-start(bf16[2,72,1152]{2,1,0:T(8,128)(2,1)S(1)} %get-tuple-element.192), channel_id=1, source_target_pairs={{0,2},{1,3},{2,0},{3,1},{4,6},{5,7},{6,4},{7,5},{8,10},{9,11},{10,... | collective-permute-start | bytes 995336 | tf_op jit(solution)/shard_map/ppermute | solution.py:677
  739.8 47.0 %collective-permute-start.83 = (bf16[2,72,1152]{2,1,0:T(8,128)(2,1)S(1)}, bf16[2,72,1152]{2,1,0:T(8,128)(2,1)S(1)}, u32[]{:S(2)}, u32[]{:S(2)}) collective-permute-start(bf16[2,72,1152]{2,1,0:T(8,128)(2,1)S(1)} %get-tuple-element.195), channel_id=1, source_target_pairs={{0,3},{1,0},{2,1},{3,2},{4,7},{5,4},{6,5},{7,6},{8,11},{9,8},{10,9... | collective-permute-start | bytes 995336 | tf_op jit(solution)/shard_map/ppermute | solution.py:677
  (122 other events, 2094.6 us)
